TPU v7x, 1024 devices: a whole 4x4x32 slice. The times are simulated.
1024 devices in a mesh: dp: 4 (over y_lo, core), expert: 32 (over z), tpin: 2 (over y_hi), tpout: 4 (over x).
Axes of the slice: x: 4, y: 4 (y_hi: 2, y_lo: 2; y = y_hi * 2 + y_lo), z: 32, core: 2. Of those that a mesh axis runs over, the one named last changes fastest.
Arguments:
- tokens: bfloat16 [512, 6144], P('expert', ('dp', 'tpin', 'tpout')), may hold values from -6 to 6
- cotangent: bfloat16 [512, 6144], P('expert', ('dp', 'tpin', 'tpout')), may hold values from -6 to 6
- expert_ids: int32 [512, 2], P('expert'), may hold values from 0 to 7, all different within a row; in each aligned block of 16 rows (0 to 15, 16 to 31, ...) at most 6 rows name the same one
- gate_weights: float32 [512, 2], P('expert'), may hold values from 0.25 to 1
- w_gate: bfloat16 [6144, 65536], P(('dp', 'tpin'), ('expert', 'tpout')), may hold values from -0.078125 to 0.078125
- w_up: bfloat16 [6144, 65536], P(('dp', 'tpin'), ('expert', 'tpout')), may hold values from -0.078125 to 0.078125
- w_down: bfloat16 [65536, 6144], P(('expert', 'tpout'), ('dp', 'tpin')), may hold values from -0.0625 to 0.0625
Outputs:
- layer_out: bfloat16 [512, 6144], P('expert', ('dp', 'tpin', 'tpout'))
- token_grad: bfloat16 [512, 6144], P('expert', ('dp', 'tpin', 'tpout'))
- down_grad: bfloat16 [65536, 6144], P(('expert', 'tpout'), ('dp', 'tpin'))
Inputs may be any that keep to these rules, and one draw needn't show every extreme that they name: `expert_ids`: each row names 2 different experts. In each aligned block of 16 rows no expert is named by more than 6 rows, a bound that some block reaches.
All inputs are finite; a program needn't handle non-finite values.
Results may differ from a plain program's by a relative error of at most 0.0057.
Values may be sent and summed in bfloat16 or wider, within the bound.
A program may use at most 64 MiB of HBM per device.

v0:
```python
import jax
import jax.numpy as jnp
from jax import lax
from jax.sharding import PartitionSpec as P

EXPERTS = 8
HID = 8192
CAP = 6


def contract_last(left, right):
    return lax.dot_general(
        left, right, (((1,), (1,)), ((), ())), preferred_element_type=jnp.float32
    )


def contract_first(left, right):
    return lax.dot_general(
        left,
        right,
        (((0,), (0,)), ((), ())),
        preferred_element_type=jnp.float32,
        precision=lax.Precision.HIGHEST,
    )


def swiglu_grads(gate, up, hidden_grad):
    sig = jax.nn.sigmoid(gate)
    hidden = (gate * sig * up).astype(jnp.bfloat16)
    gate_grad = (hidden_grad * up * sig * (1.0 + gate * (1.0 - sig))).astype(jnp.bfloat16)
    up_grad = (hidden_grad * gate * sig).astype(jnp.bfloat16)
    return (hidden, gate_grad, up_grad)


def per_device(tokens, cotangent, expert_ids, gate_weights, w_gate, w_up, w_down):
    expert_count = lax.axis_size("expert")
    outer_count = lax.axis_size("tpout")
    tok_rows, feat_cols = tokens.shape
    wide_cols, unit_cols = w_gate.shape
    block_w = unit_cols * outer_count
    per_block = max(1, block_w // HID)
    slot_count = per_block * CAP
    send_rows = expert_count * slot_count
    route_total = tok_rows * expert_ids.shape[1]
    flat_ids = expert_ids.reshape(route_total)
    onehot = (flat_ids[:, None] == jnp.arange(EXPERTS, dtype=jnp.int32)[None, :]).astype(jnp.int32)
    earlier = jnp.cumsum(onehot, axis=0) - onehot
    slot_rank = jnp.sum(earlier * onehot, axis=1)
    route_key = (flat_ids * CAP + slot_rank).reshape(expert_ids.shape)
    dest_index = jnp.arange(expert_count, dtype=jnp.int32)[:, None, None]
    group_index = jnp.arange(per_block, dtype=jnp.int32)[None, :, None]
    column = jnp.arange(CAP, dtype=jnp.int32)[None, None, :]
    target = ((dest_index * block_w // HID + group_index) * CAP + column).reshape(send_rows)
    route_match = route_key[None, :, :] == target[:, None, None]
    chosen = jnp.any(route_match, axis=2).astype(jnp.bfloat16)
    slot_weights = jnp.sum(jnp.where(route_match, gate_weights[None, :, :], 0.0), axis=2)
    slot_gate = jnp.sum(slot_weights, axis=1)
    x_send = jnp.dot(chosen, tokens, preferred_element_type=jnp.float32).astype(jnp.bfloat16)
    dy_pick = jnp.dot(chosen, cotangent, preferred_element_type=jnp.float32)
    dy_send = (slot_gate[:, None] * dy_pick).astype(jnp.bfloat16)
    x_recv, dy_recv = (
        lax.all_to_all(
            x_send.reshape(expert_count, slot_count, feat_cols),
            "expert",
            split_axis=0,
            concat_axis=0,
            tiled=True,
        ),
        lax.all_to_all(
            dy_send.reshape(expert_count, slot_count, feat_cols),
            "expert",
            split_axis=0,
            concat_axis=0,
            tiled=True,
        ),
    )
    x_all, dy_all = (
        lax.all_gather(x_recv, "tpout", axis=2, tiled=True),
        lax.all_gather(dy_recv, "tpout", axis=2, tiled=True),
    )
    expert_index = lax.axis_index("expert")
    outer_index = lax.axis_index("tpout")
    my_expert = (expert_index * outer_count + outer_index) * unit_cols // HID
    my_group = my_expert - expert_index * block_w // HID
    group_rows = expert_count * CAP

    def pick_group(whole):
        split = whole.reshape(expert_count, per_block, CAP, wide_cols)
        return split.reshape(group_rows, wide_cols)

    x_rows = pick_group(x_all)
    dy_rows = pick_group(dy_all)
    gate, up, hidden_grad = lax.psum(
        (
            jnp.dot(x_rows, w_gate, preferred_element_type=jnp.float32),
            jnp.dot(x_rows, w_up, preferred_element_type=jnp.float32),
            contract_last(dy_rows, w_down),
        ),
        ("dp", "tpin"),
    )
    hidden, gate_grad, up_grad = swiglu_grads(gate, up, hidden_grad)
    down_grad = lax.dot_general(
        hidden, dy_rows, (((0,), (0,)), ((), ())), preferred_element_type=jnp.float32
    ).astype(jnp.bfloat16)
    out_rows = jnp.dot(hidden, w_down, preferred_element_type=jnp.float32)
    grad_rows = contract_last(gate_grad, w_gate) + contract_last(up_grad, w_up)

    def widen_rows(rows):
        placed = rows.reshape(expert_count, 1, CAP, wide_cols)
        return placed.reshape(expert_count, slot_count, wide_cols)

    out_back, grad_back = (
        lax.psum_scatter(widen_rows(out_rows), "tpout", scatter_dimension=2, tiled=True),
        lax.psum_scatter(widen_rows(grad_rows), "tpout", scatter_dimension=2, tiled=True),
    )
    out_home, grad_home = (
        lax.all_to_all(out_back, "expert", split_axis=0, concat_axis=0, tiled=True),
        lax.all_to_all(grad_back, "expert", split_axis=0, concat_axis=0, tiled=True),
    )
    layer_out = contract_first(slot_weights, out_home.reshape(send_rows, feat_cols)).astype(
        jnp.bfloat16
    )
    token_grad = contract_first(
        chosen.astype(jnp.float32), grad_home.reshape(send_rows, feat_cols)
    ).astype(jnp.bfloat16)
    return (layer_out, token_grad, down_grad)


def solution(mesh):
    return jax.shard_map(
        per_device,
        mesh=mesh,
        in_specs=(
            P("expert", ("dp", "tpin", "tpout")),
            P("expert", ("dp", "tpin", "tpout")),
            P("expert", None),
            P("expert", None),
            P(("dp", "tpin"), ("expert", "tpout")),
            P(("dp", "tpin"), ("expert", "tpout")),
            P(("expert", "tpout"), ("dp", "tpin")),
        ),
        out_specs=(
            P("expert", ("dp", "tpin", "tpout")),
            P("expert", ("dp", "tpin", "tpout")),
            P(("expert", "tpout"), ("dp", "tpin")),
        ),
        check_vma=False,
    )
```

profile of v0, /device:TPU:1, one launch (start us, length us, event | category | flops | bytes accessed | tf_op | source)
XLA Modules:
  0.0 404.3 jit_solution(604266407398624691)
XLA Ops:
  7.2 0.8 copy.34
  8.2 0.2 select_reduce_fusion.2
  8.5 0.1 copy.35
  8.6 0.7 multiply_add_fusion
  9.4 0.1 add.56
  9.6 0.8 select_reduce_fusion
  10.3 0.9 fusion
  11.3 0.7 reshape.90
  11.9 29.3 %all-to-all-start.2 = ((bf16[32,6,192]{2,1,0:T(8,128)(2,1)}), bf16[32,6,192]{2,1,0:T(8,128)(2,1)S(1)}, u32[]{:S(2)}, u32[]{:S(2)}) async-start(bf16[32,6,192]{2,1,0:T(8,128)(2,1)} %reshape.90), calls=%async_computation.2 | async-start | bytes 262144 | tf_op jit(solution)/shard_map/all_to_all | solution.py:69
  41.2 0.9 convolution_convert_fusion.1
  42.2 0.7 reshape.88
  42.9 28.0 %all-to-all-done.2 = bf16[32,6,192]{2,1,0:T(8,128)(2,1)S(1)} async-done(((bf16[32,6,192]{2,1,0:T(8,128)(2,1)}), bf16[32,6,192]{2,1,0:T(8,128)(2,1)S(1)}, u32[]{:S(2)}, u32[]{:S(2)}) %all-to-all-start.2) | async-done | bytes 73760 | tf_op jit(solution)/shard_map/all_to_all | solution.py:69
  70.8 3.9 all-to-all-start
  74.7 0.3 copy.38
  75.0 15.8 %all_gather.7 = bf16[32,6,768]{0,1,2:T(8,128)(2,1)S(1)} all-gather(bf16[32,6,192]{0,1,2:T(8,128)(2,1)S(1)} %copy.38), channel_id=1, replica_groups=mesh['dp'=4,'expert'=32,'tpin'=2,'tpout'=4] {'tpout'}, dimensions={2}, use_global_device_ids=true | all-gather | bytes 368640 | tf_op jit(solution)/shard_map/all_gather | solution.py:79
  90.8 1.1 copy.39
  91.9 0.1 reshape_reshape.14
  92.0 9.4 %all-to-all-done = bf16[32,6,192]{2,1,0:T(8,128)(2,1)S(1)} async-done(((bf16[32,6,192]{2,1,0:T(8,128)(2,1)}), bf16[32,6,192]{2,1,0:T(8,128)(2,1)S(1)}, u32[]{:S(2)}, u32[]{:S(2)}) %all-to-all-start) | async-done | bytes 73760 | tf_op jit(solution)/shard_map/all_to_all | solution.py:62
  101.4 0.3 copy.36
  101.7 14.7 %all_gather.6 = bf16[32,6,768]{0,1,2:T(8,128)(2,1)S(1)} all-gather(bf16[32,6,192]{0,1,2:T(8,128)(2,1)S(1)} %copy.36), channel_id=1, replica_groups=mesh['dp'=4,'expert'=32,'tpin'=2,'tpout'=4] {'tpout'}, dimensions={2}, use_global_device_ids=true | all-gather | bytes 368640 | tf_op jit(solution)/shard_map/all_gather | solution.py:78
  116.4 1.7 copy.37
  118.1 1.1 reshape_reshape.12
  119.2 1.1 fusion.8
  120.2 2.2 fusion.9
  122.5 1.1 fusion.11
  123.7 94.9 %all-reduce.3.cloned.1.call-done = (f32[192,512]{1,0:T(8,128)}, f32[192,512]{1,0:T(8,128)}, f32[192,512]{1,0:T(8,128)}) async-done(((f32[192,512]{1,0:T(8,128)}, f32[192,512]{1,0:T(8,128)}, f32[192,512]{1,0:T(8,128)}), (f32[192,512]{1,0:T(8,128)}, f32[192,512]{1,0:T(8,128)}, f32[192,512]{1,0:T(8,128)})) %all-reduce.3.cloned.1.call-update) | async-done | bytes 1179664 | tf_op jit(solution)/shard_map/psum | solution.py:93
  218.5 1.7 fusion.1
  220.3 1.5 convolution_add_fusion
  221.9 10.6 %copy.42 = f32[32,6,768]{1,0,2:T(8,128)} copy(f32[32,6,768]{2,1,0:T(8,128)S(1)} %reshape_reshape.15) | data formatting | bytes 1179648
  232.5 12.2 %reshape.94 = f32[768,192]{1,0:T(8,128)} reshape(f32[768,32,6]{2,1,0:T(8,128)} %bitcast.28) | data formatting | bytes 1179648
  244.7 0.2 reduce-scatter.7.cloned.1.call-start
  244.9 0.1 multiply_convert_fusion.2
  245.1 0.3 fusion.10
  245.5 10.6 %copy.40 = f32[32,6,768]{1,0,2:T(8,128)} copy(f32[32,6,768]{2,1,0:T(8,128)S(1)} %reshape_reshape.13) | data formatting | bytes 1179648
  256.1 12.1 %reshape.92 = f32[768,192]{1,0:T(8,128)} reshape(f32[768,32,6]{2,1,0:T(8,128)} %bitcast.29) | data formatting | bytes 1179648
  268.2 14.9 %reduce-scatter.9.cloned.1.call-done = f32[192,192]{1,0:T(8,128)} async-done(((f32[768,192]{1,0:T(8,128)}), f32[192,192]{1,0:T(8,128)}) %reduce-scatter.9.cloned.1.call-update) | async-done | bytes 147472
  283.1 5.2 %reshape.95 = f32[192,32,6]{2,1,0:T(8,128)} reshape(f32[192,192]{1,0:T(8,128)} %reduce-scatter.9.cloned.1.call-done) | data formatting | bytes 294912
  288.4 3.6 copy.43
  291.9 22.4 %all-to-all-start.3 = ((f32[32,6,192]{2,1,0:T(8,128)}), f32[32,6,192]{2,1,0:T(8,128)S(1)}, u32[]{:S(2)}, u32[]{:S(2)}) async-start(f32[32,6,192]{2,1,0:T(8,128)} %copy.43), calls=%async_computation.3 | async-start | bytes 524288 | tf_op jit(solution)/shard_map/all_to_all | solution.py:118
  314.3 13.3 %reduce-scatter.7.cloned.1.call-done = f32[192,192]{1,0:T(8,128)} async-done(((f32[768,192]{1,0:T(8,128)}), f32[192,192]{1,0:T(8,128)}) %reduce-scatter.7.cloned.1.call-update) | async-done | bytes 147472
  327.6 5.2 %reshape.93 = f32[192,32,6]{2,1,0:T(8,128)} reshape(f32[192,192]{1,0:T(8,128)} %reduce-scatter.7.cloned.1.call-done) | data formatting | bytes 294912
  332.8 3.6 copy.41
  336.4 15.9 %all-to-all-done.3 = f32[32,6,192]{2,1,0:T(8,128)S(1)} async-done(((f32[32,6,192]{2,1,0:T(8,128)}), f32[32,6,192]{2,1,0:T(8,128)S(1)}, u32[]{:S(2)}, u32[]{:S(2)}) %all-to-all-start.3) | async-done | bytes 147488 | tf_op jit(solution)/shard_map/all_to_all | solution.py:118
  352.3 6.7 %all-to-all-start.1 = ((f32[32,6,192]{2,1,0:T(8,128)}), f32[32,6,192]{2,1,0:T(8,128)S(1)}, u32[]{:S(2)}, u32[]{:S(2)}) async-start(f32[32,6,192]{2,1,0:T(8,128)} %copy.41), calls=%async_computation.1 | async-start | bytes 524288 | tf_op jit(solution)/shard_map/all_to_all | solution.py:117
  359.0 1.3 convolution_convert_fusion
  360.3 0.8 convolution_convert_fusion.2
  361.1 35.8 %all-to-all-done.1 = f32[32,6,192]{2,1,0:T(8,128)S(1)} async-done(((f32[32,6,192]{2,1,0:T(8,128)}), f32[32,6,192]{2,1,0:T(8,128)S(1)}, u32[]{:S(2)}, u32[]{:S(2)}) %all-to-all-start.1) | async-done | bytes 147488 | tf_op jit(solution)/shard_map/all_to_all | solution.py:117
  397.0 0.8 convolution_convert_fusion.3
  (26 shorter events, 0.8 us)
Async XLA Ops:
  7.2 112.0 %copy-start = (bf16[768,512]{1,0:T(8,128)(2,1)S(1)}, bf16[768,512]{1,0:T(8,128)(2,1)}, u32[]{:S(2)}) copy-start(bf16[768,512]{1,0:T(8,128)(2,1)} %param.11) | copy-start | bytes 2359300
  11.9 58.9 %all-to-all-start.2 = ((bf16[32,6,192]{2,1,0:T(8,128)(2,1)}), bf16[32,6,192]{2,1,0:T(8,128)(2,1)S(1)}, u32[]{:S(2)}, u32[]{:S(2)}) async-start(bf16[32,6,192]{2,1,0:T(8,128)(2,1)} %reshape.90), calls=%async_computation.2 | async-start | bytes 262144 | tf_op jit(solution)/shard_map/all_to_all | solution.py:69
  70.8 30.6 %all-to-all-start = ((bf16[32,6,192]{2,1,0:T(8,128)(2,1)}), bf16[32,6,192]{2,1,0:T(8,128)(2,1)S(1)}, u32[]{:S(2)}, u32[]{:S(2)}) async-start(bf16[32,6,192]{2,1,0:T(8,128)(2,1)} %reshape.88), calls=%async_computation | async-start | bytes 262144 | tf_op jit(solution)/shard_map/all_to_all | solution.py:62
  74.7 143.9 %all-reduce.3.cloned.1.call-start = ((), (), s32[]{:S(2)}) async-start(), calls=%async_computation.8 | async-start | bytes 2359296 | tf_op jit(solution)/shard_map/psum | solution.py:93
  116.4 6.1 %copy-start.1 = (bf16[512,768]{1,0:T(8,128)(2,1)S(1)}, bf16[512,768]{1,0:T(8,128)(2,1)}, u32[]{:S(2)}) copy-start(bf16[512,768]{1,0:T(8,128)(2,1)} %param.13) | copy-start | bytes 2359300
  122.5 97.8 %copy-start.2 = (bf16[768,512]{1,0:T(8,128)(2,1)S(1)}, bf16[768,512]{1,0:T(8,128)(2,1)}, u32[]{:S(2)}) copy-start(bf16[768,512]{1,0:T(8,128)(2,1)} %param.12) | copy-start | bytes 2359300
  123.6 159.5 %reduce-scatter.9.cloned.1.call-start = ((), (), s32[]{:S(2)}) async-start(), calls=%async_computation.7 | async-start | bytes 983040
  232.5 12.4 %copy-start.3 = (f32[192,512]{1,0:T(8,128)S(1)}, f32[192,512]{1,0:T(8,128)}, u32[]{:S(2)}) copy-start(f32[192,512]{1,0:T(8,128)} %get-tuple-element.6) | copy-start | bytes 1179652
  232.5 12.4 %copy-start.4 = (f32[192,512]{1,0:T(8,128)S(1)}, f32[192,512]{1,0:T(8,128)}, u32[]{:S(2)}) copy-start(f32[192,512]{1,0:T(8,128)} %get-tuple-element.5) | copy-start | bytes 1179652
  244.7 82.9 %reduce-scatter.7.cloned.1.call-start = ((), (), s32[]{:S(2)}) async-start(), calls=%async_computation.6 | async-start | bytes 983040
  291.9 60.3 %all-to-all-start.3 = ((f32[32,6,192]{2,1,0:T(8,128)}), f32[32,6,192]{2,1,0:T(8,128)S(1)}, u32[]{:S(2)}, u32[]{:S(2)}) async-start(f32[32,6,192]{2,1,0:T(8,128)} %copy.43), calls=%async_computation.3 | async-start | bytes 524288 | tf_op jit(solution)/shard_map/all_to_all | solution.py:118
  352.3 44.7 %all-to-all-start.1 = ((f32[32,6,192]{2,1,0:T(8,128)}), f32[32,6,192]{2,1,0:T(8,128)S(1)}, u32[]{:S(2)}, u32[]{:S(2)}) async-start(f32[32,6,192]{2,1,0:T(8,128)} %copy.41), calls=%async_computation.1 | async-start | bytes 524288 | tf_op jit(solution)/shard_map/all_to_all | solution.py:117
Sparse Core Ops, SparseCore 0:
  123.7 94.7 all-reduce.2
  244.8 38.2 reduce-scatter.8
  287.1 40.3 reduce-scatter.6
where the time goes:
time: 409 us; the launch traced here: 404 us
  waiting for transfers between devices  212 us (52%)
  local copies, waits for them, and re-layouts  70.4 us (17%)
  starting transfers between devices  62.5 us (15%)
  blocking collectives  30.5 us (7%)
  between operations  13.9 us (3%)
  matrix products  12.7 us (3%)
    psum x1, waiting for transfers between devices, per_device(): lax.psum((jnp.dot(x_rows, w_gate, preferred_element_type=jnp.float32), jn...  94.9 us
    unnamed x19, local copies, waits for them, and re-layouts  63.9 us
    all_to_all x1, waiting for transfers between devices, per_device(): lax.all_to_all(out_back, 'expert', split_axis=0, concat_axis=0, tiled=True)  35.8 us
    all_to_all x1, starting transfers between devices, per_device(): lax.all_to_all(dy_send.reshape(expert_count, slot_count, feat_cols), 'exp...  29.3 us
    unnamed x5, waiting for transfers between devices  28.2 us
    all_to_all x1, waiting for transfers between devices, per_device(): lax.all_to_all(dy_send.reshape(expert_count, slot_count, feat_cols), 'exp...  28 us
    all_to_all x1, starting transfers between devices, per_device(): lax.all_to_all(grad_back, 'expert', split_axis=0, concat_axis=0, tiled=True)  22.4 us
    all_to_all x1, waiting for transfers between devices, per_device(): lax.all_to_all(grad_back, 'expert', split_axis=0, concat_axis=0, tiled=True)  15.9 us
  transfers between devices with their start and end apart: 7, of which 7 were waited for; matrix products, arithmetic and copies ran while one was open for 11% of the time, Pallas kernels for 0%

commit v1 on v0

v1 whole, which is shorter than its diff:
```python
import jax
import jax.numpy as jnp
from jax import lax
from jax.experimental import pallas as pl
from jax.experimental.pallas import tpu as pltpu
from jax.sharding import PartitionSpec as P

EXPERTS = 8
HID = 8192
CAP = 6
SLOT = 8
MESH = pl.DeviceIdType.MESH
F32 = jnp.float32
BF16 = jnp.bfloat16

HOPS = (0, 1, 2, 3, 4, 3, 2, 1)
AHEAD = (0, 1, 1, 1, 0, -1, -1, -1)
FIRST = (4, 3, 5, 2, 6, 1, 7)
RELAYS = tuple((k, h) for h in (1, 2, 3) for k in (4, 3, 5, 2, 6) if HOPS[k] > h)
ARRIVALS = tuple((k, h) for k in range(1, 8) for h in range(1, HOPS[k] + 1))


def dot(a, b, contract=((1,), (0,)), precision=None):
    return lax.dot_general(
        a, b, (contract, ((), ())), preferred_element_type=F32, precision=precision
    )


def kernel(
    ids_ref, gw_ref, tok_ref, cot_ref, wg_hbm, wu_hbm, wd_hbm,
    out_ref, grad_ref, down_hbm,
    wg, wu, wd, w_sem,
    a_src, a_relay, a_dst, a_send, a_recv,
    xg, b_zsend, b_zrecv, b_xsend, b_xrecv,
    p_mine, d1_src, d1_dst, d1_send, d1_recv,
    d2_src, d2_dst, d2_send, d2_recv,
    h_all, d3_send, d3_recv, d4_send, d4_recv,
    f_mine, f_src, f_dst, f_send, f_recv,
    z_src, z_dst, z_send, z_recv,
    g_src, g_dst, g_send, g_recv,
    down_buf, down_sem,
):
    z = lax.axis_index("expert")
    x = lax.axis_index("tpout")
    y_hi = lax.axis_index("tpin")
    dp = lax.axis_index("dp")
    planes = lax.axis_size("expert") // EXPERTS
    group, plane = z // planes, z % planes
    core = dp % 2
    y = y_hi * 2 + dp // 2
    side = 1 - 2 * core
    xs = lax.axis_size("tpout")

    def at_group(step):
        return {"expert": ((group + step + EXPERTS) % EXPERTS) * planes + plane}

    def at_plane(p):
        return {"expert": group * planes + p}

    def at_x(step):
        return {"tpout": (x + step + xs) % xs}

    def at_y(step):
        there = (y + step + 4) % 4
        return {"tpin": there // 2, "dp": (there % 2) * 2 + core}

    partner = {"dp": dp + side}
    near_planes = (plane + 1 - 2 * (plane % 2), (plane + 2) % 4, 3 - plane)

    def remote(src, dst, send, recv, device):
        return pltpu.make_async_remote_copy(
            src_ref=src, dst_ref=dst, send_sem=send, recv_sem=recv,
            device_id=device, device_id_type=MESH,
        )

    barrier = pltpu.get_barrier_semaphore()
    peers = [at_group(1), at_group(-1), at_x(1), at_x(-1), at_y(1), at_y(-1), partner]
    peers += [at_plane(p) for p in near_planes]
    for peer in peers:
        pl.semaphore_signal(barrier, inc=1, device_id=peer, device_id_type=MESH)
    weights = [
        pltpu.make_async_copy(src, dst, w_sem.at[i])
        for i, (src, dst) in enumerate(((wg_hbm, wg), (wu_hbm, wu), (wd_hbm, wd)))
    ]
    for copy in weights:
        copy.start()

    ahead = (ids_ref[...] + EXPERTS - group) % EXPERTS
    gw = gw_ref[...]
    tokens_n = ahead.shape[1]
    expert_row = lax.broadcasted_iota(jnp.int32, (EXPERTS, tokens_n), 0)
    hit0 = jnp.where(expert_row == ahead[0:1, :], 1.0, 0.0).astype(F32)
    hit1 = jnp.where(expert_row == ahead[1:2, :], 1.0, 0.0).astype(F32)
    hit = hit0 + hit1
    weight = hit0 * gw[0:1, :] + hit1 * gw[1:2, :]
    before = jnp.where(
        lax.broadcasted_iota(jnp.int32, (tokens_n, tokens_n), 0)
        < lax.broadcasted_iota(jnp.int32, (tokens_n, tokens_n), 1), 1.0, 0.0
    ).astype(F32)
    rank = dot(hit, before)

    def spread(v):
        return jnp.concatenate(
            [jnp.broadcast_to(v[e : e + 1, :], (SLOT, tokens_n)) for e in range(EXPERTS)], axis=0
        )

    slots_n = EXPERTS * SLOT
    slot_j = (lax.broadcasted_iota(jnp.int32, (slots_n, tokens_n), 0) % SLOT).astype(F32)
    chosen = jnp.where(spread(rank) == slot_j, spread(hit), 0.0)
    slot_weights = chosen * spread(weight)
    chosen_b = chosen.astype(BF16)
    slot_gate = jnp.sum(slot_weights, axis=1, keepdims=True)
    x_rows = dot(chosen_b, tok_ref[...])
    dy_rows = dot(chosen_b, cot_ref[...]) * slot_gate
    feat = x_rows.shape[1]
    both = jnp.concatenate([x_rows, dy_rows], axis=1)
    a_src[...] = both.reshape(EXPERTS, SLOT, 2 * feat).astype(BF16)
    a_dst[0] = a_src[0]

    pl.semaphore_wait(barrier, len(peers))

    def a_copy(k, h):
        src = a_src.at[k] if h == 1 else a_relay.at[RELAYS.index((k, h - 1))]
        dst = a_dst.at[k] if h == HOPS[k] else a_relay.at[RELAYS.index((k, h))]
        n = ARRIVALS.index((k, h))
        step = side if k == 4 else AHEAD[k]
        return remote(src, dst, a_send.at[n], a_recv.at[n], at_group(step))

    for k in FIRST:
        a_copy(k, 1).start()
    chosen_t = chosen.T
    weights_t = slot_weights.T
    for k, h in RELAYS:
        a_copy(k, h).wait_recv()
        a_copy(k, h + 1).start()
    for k in range(1, 8):
        a_copy(k, HOPS[k]).wait_recv()

    cap_rows = EXPERTS * CAP

    def squeeze(shape, long_axis):
        rows = lax.broadcasted_iota(jnp.int32, shape, long_axis)
        short = lax.broadcasted_iota(jnp.int32, shape, 1 - long_axis)
        return jnp.where(short // CAP * SLOT + short % CAP == rows, 1.0, 0.0).astype(BF16)

    arrived = a_dst[...].reshape(slots_n, 2 * feat)
    xg[x, plane] = dot(squeeze((cap_rows, slots_n), 1), arrived).astype(BF16)

    order = (plane,) + near_planes

    def bz_out(j):
        mine = xg.at[x, plane]
        return remote(mine, mine, b_zsend.at[j - 1], b_zrecv.at[j - 1], at_plane(order[j]))

    def bz_in(j):
        there = xg.at[x, order[j]]
        return remote(there, there, b_zsend.at[j - 1], b_zrecv.at[j - 1], at_plane(order[j]))

    def bx_out(j, way):
        mine = xg.at[x, order[j]]
        n = 0 if way == 1 else 1
        return remote(mine, mine, b_xsend.at[j, n], b_xrecv.at[j, n], at_x(way))

    def bx_in(j, way):
        there = xg.at[(x - way + xs) % xs, order[j]]
        n = 0 if way == 1 else 1
        return remote(there, there, b_xsend.at[j, n], b_xrecv.at[j, n], at_x(way))

    def bx_pass(j):
        way = 1 if j < 2 else -1
        there = xg.at[(x - way + xs) % xs, order[j]]
        return remote(there, there, b_xsend.at[j, 2], b_xrecv.at[j, 2], at_x(way))

    def bx_far(j):
        there = xg.at[(x + 2) % xs, order[j]]
        return remote(there, there, b_xsend.at[j, 2], b_xrecv.at[j, 2], at_x(1))

    for j in (1, 2, 3):
        bz_out(j).start()
    for way in (1, -1):
        bx_out(0, way).start()

    def relay_x(j):
        bx_in(j, 1 if j < 2 else -1).wait_recv()
        bx_pass(j).start()

    for j in (1, 2, 3):
        bz_in(j).wait_recv()
        for way in (1, -1):
            bx_out(j, way).start()
        relay_x(j - 1)
    relay_x(3)
    for copy in weights:
        copy.wait()
    for j in range(4):
        bx_in(j, -1 if j < 2 else 1).wait_recv()
        bx_far(j).wait_recv()

    rows_n = planes * cap_rows
    half = rows_n // 2
    blocks = [xg[i].reshape(rows_n, 2 * feat) for i in range(4)]
    x_all = jnp.concatenate([b[:, :feat] for b in blocks], axis=1)
    dy_all = jnp.concatenate([b[:, feat:] for b in blocks], axis=1)
    parts = (
        dot(x_all, wg[...]),
        dot(x_all, wu[...]),
        dot(dy_all, wd[...], ((1,), (1,))),
    )
    for i in range(4):
        for n, part in enumerate(parts):
            p_mine[i, :, n * 128 : (n + 1) * 128] = part[:, i * 128 : (i + 1) * 128]

    my_rows = pl.ds(pl.multiple_of(core * half, half), half)
    its_rows = pl.ds(pl.multiple_of((1 - core) * half, half), half)

    def d1(i):
        return remote(d1_src.at[i], d1_dst.at[i], d1_send.at[i], d1_recv.at[i], partner)

    wrap_y = [(y + step) % 4 for step in range(4)]
    for step in (2, 1, 3, 0):
        d1_src[step] = p_mine[wrap_y[step], its_rows, :].astype(BF16)
        d1(step).start()

    quarter = half // 2
    top, bottom = pl.ds(0, quarter), pl.ds(quarter, quarter)

    def d2(n, way):
        return remote(d2_src.at[n], d2_dst.at[n], d2_send.at[n], d2_recv.at[n], at_y(way))

    def pair_sum(step):
        d1(step).wait_recv()
        return p_mine[wrap_y[step], my_rows, :] + d1_dst[step].astype(F32)

    far = pair_sum(2).astype(BF16)
    d2_src[0] = far[:quarter]
    d2(0, 1).start()
    d2_src[1] = far[quarter:]
    d2(1, -1).start()
    ahead_sum = pair_sum(1)
    d2_src[2] = ahead_sum[quarter:].astype(BF16)
    d2(2, 1).start()
    back_sum = pair_sum(3)
    d2_src[3] = back_sum[:quarter].astype(BF16)
    d2(3, -1).start()
    mine = pair_sum(0)
    d2(0, 1).wait_recv()
    d2_src[4] = (ahead_sum[:quarter] + d2_dst[0].astype(F32)).astype(BF16)
    d2(4, 1).start()
    d2(1, -1).wait_recv()
    d2_src[5] = (back_sum[quarter:] + d2_dst[1].astype(F32)).astype(BF16)
    d2(5, -1).start()
    for n, way in ((2, 1), (3, -1), (4, 1), (5, -1)):
        d2(n, way).wait_recv()
    from_back = jnp.concatenate([d2_dst[4], d2_dst[2]], axis=0).astype(F32)
    from_ahead = jnp.concatenate([d2_dst[3], d2_dst[5]], axis=0).astype(F32)
    total = mine + from_back + from_ahead

    gate, up, hidden_grad = total[:, :128], total[:, 128:256], total[:, 256:]
    sig = 1.0 / (1.0 + jnp.exp(-gate))
    hidden = (gate * sig * up).astype(BF16)
    gate_grad = (hidden_grad * up * sig * (1.0 + gate * (1.0 - sig))).astype(BF16)
    up_grad = (hidden_grad * gate * sig).astype(BF16)
    h_all[y, core] = jnp.concatenate([hidden, gate_grad, up_grad], axis=1)

    def d3_out(way):
        own = h_all.at[y, core]
        n = 0 if way == 1 else 1
        return remote(own, own, d3_send.at[n], d3_recv.at[n], at_y(way))

    def d3_in(way):
        there = h_all.at[(y - way + 4) % 4, core]
        n = 0 if way == 1 else 1
        return remote(there, there, d3_send.at[n], d3_recv.at[n], at_y(way))

    def d3_pass(way):
        n, rows = (2, top) if way == 1 else (3, bottom)
        there = h_all.at[(y - way + 4) % 4, core, rows]
        return remote(there, there, d3_send.at[n], d3_recv.at[n], at_y(way))

    def d3_far(way):
        n, rows = (2, top) if way == 1 else (3, bottom)
        there = h_all.at[(y + 2) % 4, core, rows]
        return remote(there, there, d3_send.at[n], d3_recv.at[n], at_y(way))

    def d4(step, whose):
        there = h_all.at[wrap_y[step], whose]
        return remote(there, there, d4_send.at[step], d4_recv.at[step], partner)

    d3_out(1).start()
    d3_out(-1).start()
    d4(0, core).start()
    d3_in(1).wait_recv()
    d3_pass(1).start()
    d3_in(-1).wait_recv()
    d3_pass(-1).start()
    d4(3, core).start()
    d4(1, core).start()
    d3_far(1).wait_recv()
    d3_far(-1).wait_recv()
    d4(2, core).start()
    for step in range(4):
        d4(step, 1 - core).wait_recv()

    acts = [h_all[i].reshape(rows_n, 384) for i in range(4)]
    hidden_all = jnp.concatenate([a[:, :128] for a in acts], axis=1)
    gate_grad_all = jnp.concatenate([a[:, 128:256] for a in acts], axis=1)
    up_grad_all = jnp.concatenate([a[:, 256:] for a in acts], axis=1)
    out_rows = dot(hidden_all, wd[...])
    grad_rows = dot(gate_grad_all, wg[...], ((1,), (1,))) + dot(
        up_grad_all, wu[...], ((1,), (1,))
    )
    for i in range(4):
        cols = slice(i * feat, (i + 1) * feat)
        f_mine[i] = jnp.concatenate([out_rows[:, cols], grad_rows[:, cols]], axis=1)

    def f(n, way):
        return remote(f_src.at[n], f_dst.at[n], f_send.at[n], f_recv.at[n], at_x(way))

    def f_part(step):
        return f_mine[(x + step) % xs]

    far = f_part(2).astype(BF16)
    f_src[0] = far[:half]
    f(0, 1).start()
    f_src[1] = far[half:]
    f(1, -1).start()
    ahead_part = f_part(1)
    f_src[2] = ahead_part[half:].astype(BF16)
    f(2, 1).start()
    back_part = f_part(3)
    f_src[3] = back_part[:half].astype(BF16)
    f(3, -1).start()
    f(0, 1).wait_recv()
    f_src[4] = (ahead_part[:half] + f_dst[0].astype(F32)).astype(BF16)
    f(4, 1).start()
    f(1, -1).wait_recv()
    f_src[5] = (back_part[half:] + f_dst[1].astype(F32)).astype(BF16)
    f(5, -1).start()
    for n, way in ((2, 1), (3, -1), (4, 1), (5, -1)):
        f(n, way).wait_recv()
    from_back = jnp.concatenate([f_dst[4], f_dst[2]], axis=0).astype(F32)
    from_ahead = jnp.concatenate([f_dst[3], f_dst[5]], axis=0).astype(F32)
    f_mine[0] = f_part(0) + from_back + from_ahead

    def zc(j):
        return remote(z_src.at[j - 1], z_dst.at[j - 1], z_send.at[j - 1], z_recv.at[j - 1], at_plane(order[j]))

    def chunk(p):
        return pl.ds(pl.multiple_of(p * cap_rows, cap_rows), cap_rows)

    for j in (2, 3, 1):
        z_src[j - 1] = f_mine[0, chunk(order[j]), :].astype(BF16)
        zc(j).start()
    routes = f_mine[0, chunk(plane), :]
    for j in (1, 3, 2):
        zc(j).wait_recv()
        routes = routes + z_dst[j - 1].astype(F32)

    wide = dot(squeeze((slots_n, cap_rows), 0), routes.astype(BF16))
    g_src[...] = wide.reshape(EXPERTS, SLOT, 2 * feat).astype(BF16)

    def gc(k, way):
        return remote(g_src.at[k], g_dst.at[k], g_send.at[k - 1], g_recv.at[k - 1], at_group(way * k))

    for k in (4, 3, 5, 2, 6, 1, 7):
        gc(k, -1).start()
    g_dst[0] = g_src[0]
    down_buf[...] = dot(hidden_all, dy_all, ((0,), (0,))).astype(BF16)
    down_copy = pltpu.make_async_copy(down_buf, down_hbm, down_sem)
    down_copy.start()
    for k in range(1, 8):
        gc(k, 1).wait_recv()
    home = g_dst[...].reshape(slots_n, 2 * feat).astype(F32)
    out_ref[...] = dot(weights_t, home[:, :feat], precision=lax.Precision.HIGHEST).astype(BF16)
    grad_ref[...] = dot(chosen_t, home[:, feat:], precision=lax.Precision.HIGHEST).astype(BF16)

    down_copy.wait()
    for k in range(1, 8):
        for h in range(1, HOPS[k] + 1):
            a_copy(k, h).wait_send()
        gc(k, -1).wait_send()
    for j in (1, 2, 3):
        bz_out(j).wait_send()
        zc(j).wait_send()
    for j in range(4):
        bx_out(j, 1).wait_send()
        bx_out(j, -1).wait_send()
        bx_pass(j).wait_send()
        d1(j).wait_send()
        d4(j, core).wait_send()
    for n in range(6):
        d2(n, 1).wait_send()
        f(n, 1).wait_send()
    for way in (1, -1):
        d3_out(way).wait_send()
        d3_pass(way).wait_send()


def per_device(tokens, cotangent, expert_ids, gate_weights, w_gate, w_up, w_down):
    tok_rows, feat = tokens.shape
    wide, units = w_gate.shape
    planes = lax.axis_size("expert") // EXPERTS
    cap_rows = EXPERTS * CAP
    rows = planes * cap_rows
    half, quarter = rows // 2, rows // 4
    vmem = pl.BlockSpec(memory_space=pltpu.VMEM)
    hbm = pl.BlockSpec(memory_space=pl.ANY)
    dma = pltpu.SemaphoreType.DMA
    block = (EXPERTS, SLOT, 2 * feat)
    return pl.pallas_call(
        kernel,
        out_shape=(
            jax.ShapeDtypeStruct((tok_rows, feat), BF16),
            jax.ShapeDtypeStruct((tok_rows, feat), BF16),
            jax.ShapeDtypeStruct((units, wide), BF16),
        ),
        in_specs=[vmem, vmem, vmem, vmem, hbm, hbm, hbm],
        out_specs=(vmem, vmem, hbm),
        scratch_shapes=[
            pltpu.VMEM((wide, units), BF16), pltpu.VMEM((wide, units), BF16),
            pltpu.VMEM((units, wide), BF16), dma((3,)),
            pltpu.VMEM(block, BF16), pltpu.VMEM((len(RELAYS),) + block[1:], BF16),
            pltpu.VMEM(block, BF16), dma((len(ARRIVALS),)), dma((len(ARRIVALS),)),
            pltpu.VMEM((4, planes, cap_rows, 2 * feat), BF16),
            dma((3,)), dma((3,)), dma((4, 3)), dma((4, 3)),
            pltpu.VMEM((4, rows, 384), F32), pltpu.VMEM((4, half, 384), BF16),
            pltpu.VMEM((4, half, 384), BF16), dma((4,)), dma((4,)),
            pltpu.VMEM((6, quarter, 384), BF16), pltpu.VMEM((6, quarter, 384), BF16),
            dma((6,)), dma((6,)),
            pltpu.VMEM((4, 2, half, 384), BF16), dma((4,)), dma((4,)), dma((4,)), dma((4,)),
            pltpu.VMEM((4, rows, 2 * feat), F32), pltpu.VMEM((6, half, 2 * feat), BF16),
            pltpu.VMEM((6, half, 2 * feat), BF16), dma((6,)), dma((6,)),
            pltpu.VMEM((3, cap_rows, 2 * feat), BF16), pltpu.VMEM((3, cap_rows, 2 * feat), BF16),
            dma((3,)), dma((3,)),
            pltpu.VMEM(block, BF16), pltpu.VMEM(block, BF16), dma((7,)), dma((7,)),
            pltpu.VMEM((units, wide), BF16), dma,
        ],
        compiler_params=pltpu.CompilerParams(collective_id=0, has_side_effects=True),
    )(expert_ids.T, gate_weights.T, tokens, cotangent, w_gate, w_up, w_down)


def solution(mesh):
    return jax.shard_map(
        per_device,
        mesh=mesh,
        in_specs=(
            P("expert", ("dp", "tpin", "tpout")),
            P("expert", ("dp", "tpin", "tpout")),
            P("expert", None),
            P("expert", None),
            P(("dp", "tpin"), ("expert", "tpout")),
            P(("dp", "tpin"), ("expert", "tpout")),
            P(("expert", "tpout"), ("dp", "tpin")),
        ),
        out_specs=(
            P("expert", ("dp", "tpin", "tpout")),
            P("expert", ("dp", "tpin", "tpout")),
            P(("expert", "tpout"), ("dp", "tpin")),
        ),
        check_vma=False,
    )
```

time: 409 us -> 102 us (0.25)
  the two profiles are of different devices: /device:TPU:1 before, /device:TPU:8 now
where the time goes in v1:
time: 102 us
  Pallas kernels  97.1 us (95%)
  local copies, waits for them, and re-layouts  3.97 us (4%)
    pallas_call x1, Pallas kernels, per_device(): pl.pallas_call(kernel, out_shape=(jax.ShapeDtypeStruct((tok_rows, feat),...  97.1 us
    unnamed x5, local copies, waits for them, and re-layouts  3.97 us

profile of v1, /device:TPU:8, one launch (start us, length us, event | category | flops | bytes accessed | tf_op | source)
XLA Modules:
  0.0 101.7 jit_solution(2639671747282259903)
XLA Ops:
  0.6 97.1 %shard_map.94 = (bf16[16,192]{1,0:T(8,128)(2,1)}, bf16[16,192]{1,0:T(8,128)(2,1)}, bf16[512,768]{1,0:T(8,128)(2,1)}) custom-call(s32[2,16]{1,0:T(2,128)} %bitcast.2, f32[2,16]{1,0:T(2,128)} %bitcast.3, bf16[16,192]{1,0:T(8,128)(2,1)} %tok_ref.1, bf16[16,192]{1,0:T(8,128)(2,1)} %cot_ref.1, bf16[768,512]{1,0:T(8,128)(2,1)} %wg_hbm.1, bf16[768,512]{1,0:T(8,128)(2,1)} %wu_hbm.1, ...), custom_call_target="tpu_custom_call" | custom-call | tf_op jit(solution)/shard_map/pallas_call | solution.py:410
  97.7 0.0 copy-start
  97.7 1.3 %copy.13 = bf16[16,192]{1,0:T(8,128)(2,1)} copy(bf16[16,192]{1,0:T(8,128)(2,1)} %get-tuple-element.6) | data formatting | bytes 12288
  99.0 0.0 copy-done
  99.0 0.6 copy.14
  99.6 2.1 %copy.15 = bf16[512,768]{1,0:T(8,128)(2,1)} copy(bf16[512,768]{1,0:T(8,128)(2,1)} %get-tuple-element.8) | data formatting | bytes 1572864
Async XLA Ops:
  97.7 1.3 %copy-start = (bf16[16,192]{1,0:T(8,128)(2,1)S(1)}, bf16[16,192]{1,0:T(8,128)(2,1)}, u32[]{:S(2)}) copy-start(bf16[16,192]{1,0:T(8,128)(2,1)} %get-tuple-element.7) | copy-start | bytes 18436

commit v2 on v1

v2 whole, which is shorter than its diff:
```python
import jax
import jax.numpy as jnp
from jax import lax
from jax.experimental import pallas as pl
from jax.experimental.pallas import tpu as pltpu
from jax.sharding import PartitionSpec as P

EXPERTS = 8
HID = 8192
CAP = 6
SLOT = 8
MESH = pl.DeviceIdType.MESH
F32 = jnp.float32
BF16 = jnp.bfloat16

HOPS = (0, 1, 2, 3, 4, 3, 2, 1)
AHEAD = (0, 1, 1, 1, 0, -1, -1, -1)
FIRST = (4, 3, 5, 2, 6, 1, 7)
RELAYS = tuple((k, h) for h in (1, 2, 3) for k in (4, 3, 5, 2, 6) if HOPS[k] > h)
PLACE = (0, 1, 3, 5, 7, 6, 4, 2)
ARRIVALS = tuple((k, h) for k in range(1, 8) for h in range(1, HOPS[k] + 1))


def dot(a, b, contract=((1,), (0,)), precision=None):
    return lax.dot_general(
        a, b, (contract, ((), ())), preferred_element_type=F32, precision=precision
    )


def kernel(
    ids_hbm, gw_hbm, tok_hbm, cot_hbm, wg_hbm, wu_hbm, wd_hbm,
    home_hbm, slots_ref, hid_hbm, dy_hbm,
    ids_ref, gw_ref, tok_ref, cot_ref, in_sem,
    wg, wu, wd, w_sem,
    a_src, a_relay, a_dst, a_send, a_recv,
    xg, b_zsend, b_zrecv, b_xsend, b_xrecv,
    p_mine, d1_src, d1_dst, d1_send, d1_recv,
    d2_src, d2_dst, d2_send, d2_recv,
    h_all, d3_send, d3_recv, d4_send, d4_recv,
    f_mine, f_src, f_dst, f_send, f_recv,
    z_sum, z_src, z_dst, z_send, z_recv,
    g_src, g_send, g_recv,
    hid_buf, dy_buf, out_sem,
):
    sent = []

    z = lax.axis_index("expert")
    x = lax.axis_index("tpout")
    y_hi = lax.axis_index("tpin")
    dp = lax.axis_index("dp")
    planes = lax.axis_size("expert") // EXPERTS
    group, plane = z // planes, z % planes
    core = dp % 2
    y = y_hi * 2 + dp // 2
    side = 1 - 2 * core
    xs = lax.axis_size("tpout")

    def at_group(step):
        return {"expert": ((group + step + EXPERTS) % EXPERTS) * planes + plane}

    def at_plane(p):
        return {"expert": group * planes + p}

    def at_x(step):
        return {"tpout": (x + step + xs) % xs}

    def at_y(step):
        there = (y + step + 4) % 4
        return {"tpin": there // 2, "dp": (there % 2) * 2 + core}

    partner = {"dp": dp + side}
    near_planes = (plane + 1 - 2 * (plane % 2), (plane + 2) % 4, 3 - plane)

    def remote(src, dst, send, recv, device):
        return pltpu.make_async_remote_copy(
            src_ref=src, dst_ref=dst, send_sem=send, recv_sem=recv,
            device_id=device, device_id_type=MESH,
        )

    def start(copy):
        copy.start()
        sent.append(copy)

    barrier = pltpu.get_barrier_semaphore()
    peers = [at_group(1), at_group(-1), at_x(1), at_x(-1), at_y(1), at_y(-1), partner]
    peers += [at_plane(p) for p in near_planes]
    for peer in peers:
        pl.semaphore_signal(barrier, inc=1, device_id=peer, device_id_type=MESH)
    inputs = [
        pltpu.make_async_copy(src, dst, in_sem.at[i])
        for i, (src, dst) in enumerate(
            ((ids_hbm, ids_ref), (gw_hbm, gw_ref), (tok_hbm, tok_ref), (cot_hbm, cot_ref))
        )
    ]
    for copy in inputs:
        copy.start()
    weights = [
        pltpu.make_async_copy(src, dst, w_sem.at[i])
        for i, (src, dst) in enumerate(((wg_hbm, wg), (wu_hbm, wu), (wd_hbm, wd)))
    ]
    for copy in weights:
        copy.start()
    for copy in inputs:
        copy.wait()

    ahead = (ids_ref[...] + EXPERTS - group) % EXPERTS
    gw = gw_ref[...]
    tokens_n = ahead.shape[1]
    expert_row = lax.broadcasted_iota(jnp.int32, (EXPERTS, tokens_n), 0)
    hit0 = jnp.where(expert_row == ahead[0:1, :], 1.0, 0.0).astype(F32)
    hit1 = jnp.where(expert_row == ahead[1:2, :], 1.0, 0.0).astype(F32)
    hit = hit0 + hit1
    weight = hit0 * gw[0:1, :] + hit1 * gw[1:2, :]
    before = jnp.where(
        lax.broadcasted_iota(jnp.int32, (tokens_n, tokens_n), 0)
        < lax.broadcasted_iota(jnp.int32, (tokens_n, tokens_n), 1), 1.0, 0.0
    ).astype(F32)
    rank = dot(hit, before)

    def spread(v):
        return jnp.concatenate(
            [jnp.broadcast_to(v[e : e + 1, :], (SLOT, tokens_n)) for e in range(EXPERTS)], axis=0
        )

    slots_n = EXPERTS * SLOT
    slot_j = (lax.broadcasted_iota(jnp.int32, (slots_n, tokens_n), 0) % SLOT).astype(F32)
    chosen = jnp.where(spread(rank) == slot_j, spread(hit), 0.0)
    slot_weights = chosen * spread(weight)
    chosen_b = chosen.astype(BF16)
    slot_gate = jnp.sum(slot_weights, axis=1, keepdims=True)
    x_rows = dot(chosen_b, tok_ref[...])
    dy_rows = dot(chosen_b, cot_ref[...]) * slot_gate
    feat = x_rows.shape[1]
    both = jnp.concatenate([x_rows, dy_rows], axis=1)
    a_src[...] = both.reshape(EXPERTS, SLOT, 2 * feat).astype(BF16)
    a_dst[0] = a_src[0]

    slots_ref[0] = slot_weights
    slots_ref[1] = chosen

    pl.semaphore_wait(barrier, len(peers))

    def a_copy(k, h):
        src = a_src.at[k] if h == 1 else a_relay.at[RELAYS.index((k, h - 1))]
        dst = a_dst.at[PLACE[k]] if h == HOPS[k] else a_relay.at[RELAYS.index((k, h))]
        n = ARRIVALS.index((k, h))
        step = side if k == 4 else AHEAD[k]
        return remote(src, dst, a_send.at[n], a_recv.at[n], at_group(step))

    def a_pass(hop):
        for k, h in RELAYS:
            if h == hop:
                a_copy(k, h).wait_recv()
                start(a_copy(k, h + 1))

    cap_rows = EXPERTS * CAP
    part_rows = cap_rows // 2

    def squeeze(shape, long_axis):
        rows = lax.broadcasted_iota(jnp.int32, shape, long_axis)
        short = lax.broadcasted_iota(jnp.int32, shape, 1 - long_axis)
        return jnp.where(short // CAP * SLOT + short % CAP == rows, 1.0, 0.0).astype(BF16)

    order = (plane,) + near_planes

    def bz(c, j, whose):
        there = xg.at[x, whose, c]
        return remote(there, there, b_zsend.at[c, j - 1], b_zrecv.at[c, j - 1], at_plane(order[j]))

    def bx(c, j, n, step, way):
        there = xg.at[(x + step + xs) % xs, order[j], c]
        return remote(there, there, b_xsend.at[c, j, n], b_xrecv.at[c, j, n], at_x(way))

    def spread_x(c, j):
        start(bx(c, j, 0, 0, 1))
        start(bx(c, j, 1, 0, -1))

    def relay_x(c, j):
        n, way = (0, 1) if j < 2 else (1, -1)
        bx(c, j, n, -way, way).wait_recv()
        start(bx(c, j, 2, -way, way))

    def gather_first(c):
        half_in = a_dst[4 * c : 4 * c + 4].reshape(slots_n // 2, 2 * feat)
        xg[x, plane, c] = dot(squeeze((part_rows, slots_n // 2), 1), half_in).astype(BF16)
        for j in (1, 2, 3):
            start(bz(c, j, plane))
        spread_x(c, 0)

    for k in FIRST:
        start(a_copy(k, 1))
    a_pass(1)
    a_pass(2)
    for k in (1, 7, 2):
        a_copy(k, HOPS[k]).wait_recv()
    gather_first(0)
    a_pass(3)
    for j in (1, 2, 3):
        bz(0, j, order[j]).wait_recv()
        spread_x(0, j)
    relay_x(0, 0)
    for k in (6, 3, 5, 4):
        a_copy(k, HOPS[k]).wait_recv()
    gather_first(1)
    for j in (1, 2, 3):
        relay_x(0, j)
    for j in (1, 2, 3):
        bz(1, j, order[j]).wait_recv()
        spread_x(1, j)
        relay_x(1, j - 1)
    relay_x(1, 3)
    for copy in weights:
        copy.wait()
    for c in (0, 1):
        for j in range(4):
            n, way = (1, -1) if j < 2 else (0, 1)
            bx(c, j, n, -way, way).wait_recv()
            bx(c, j, 2, 2, 1).wait_recv()

    rows_n = planes * cap_rows
    half = rows_n // 2
    blocks = [xg[i].reshape(rows_n, 2 * feat) for i in range(4)]
    x_all = jnp.concatenate([b[:, :feat] for b in blocks], axis=1)
    dy_all = jnp.concatenate([b[:, feat:] for b in blocks], axis=1)
    dy_buf[...] = dy_all
    dy_copy = pltpu.make_async_copy(dy_buf, dy_hbm, out_sem.at[0])
    dy_copy.start()
    parts = (
        dot(x_all, wg[...]),
        dot(x_all, wu[...]),
        dot(dy_all, wd[...], ((1,), (1,))),
    )
    for i in range(4):
        for n, part in enumerate(parts):
            p_mine[i, :, n * 128 : (n + 1) * 128] = part[:, i * 128 : (i + 1) * 128]

    my_rows = pl.ds(pl.multiple_of(core * half, half), half)
    its_rows = pl.ds(pl.multiple_of((1 - core) * half, half), half)

    def d1(i):
        return remote(d1_src.at[i], d1_dst.at[i], d1_send.at[i], d1_recv.at[i], partner)

    wrap_y = [(y + step) % 4 for step in range(4)]
    for step in (2, 1, 3, 0):
        d1_src[step] = p_mine[wrap_y[step], its_rows, :]
        start(d1(step))

    quarter = half // 2
    top, bottom = pl.ds(0, quarter), pl.ds(quarter, quarter)

    def d2(n, way):
        return remote(d2_src.at[n], d2_dst.at[n], d2_send.at[n], d2_recv.at[n], at_y(way))

    def pair_sum(step):
        d1(step).wait_recv()
        return p_mine[wrap_y[step], my_rows, :] + d1_dst[step]

    far = pair_sum(2).astype(BF16)
    d2_src[0] = far[:quarter]
    start(d2(0, 1))
    d2_src[1] = far[quarter:]
    start(d2(1, -1))
    ahead_sum = pair_sum(1)
    d2_src[2] = ahead_sum[quarter:].astype(BF16)
    start(d2(2, 1))
    back_sum = pair_sum(3)
    d2_src[3] = back_sum[:quarter].astype(BF16)
    start(d2(3, -1))
    mine = pair_sum(0)
    d2(0, 1).wait_recv()
    d2_src[4] = (ahead_sum[:quarter] + d2_dst[0].astype(F32)).astype(BF16)
    start(d2(4, 1))
    d2(1, -1).wait_recv()
    d2_src[5] = (back_sum[quarter:] + d2_dst[1].astype(F32)).astype(BF16)
    start(d2(5, -1))
    for n, way in ((2, 1), (3, -1), (4, 1), (5, -1)):
        d2(n, way).wait_recv()
    from_back = jnp.concatenate([d2_dst[4], d2_dst[2]], axis=0).astype(F32)
    from_ahead = jnp.concatenate([d2_dst[3], d2_dst[5]], axis=0).astype(F32)
    total = mine + from_back + from_ahead

    gate, up, hidden_grad = total[:, :128], total[:, 128:256], total[:, 256:]
    sig = 1.0 / (1.0 + jnp.exp(-gate))
    hidden = (gate * sig * up).astype(BF16)
    gate_grad = (hidden_grad * up * sig * (1.0 + gate * (1.0 - sig))).astype(BF16)
    up_grad = (hidden_grad * gate * sig).astype(BF16)
    h_all[y, core] = jnp.concatenate([hidden, gate_grad, up_grad], axis=1)

    def d3_out(way):
        own = h_all.at[y, core]
        n = 0 if way == 1 else 1
        return remote(own, own, d3_send.at[n], d3_recv.at[n], at_y(way))

    def d3_in(way):
        there = h_all.at[(y - way + 4) % 4, core]
        n = 0 if way == 1 else 1
        return remote(there, there, d3_send.at[n], d3_recv.at[n], at_y(way))

    def d3_pass(way):
        n, rows = (2, top) if way == 1 else (3, bottom)
        there = h_all.at[(y - way + 4) % 4, core, rows]
        return remote(there, there, d3_send.at[n], d3_recv.at[n], at_y(way))

    def d3_far(way):
        n, rows = (2, top) if way == 1 else (3, bottom)
        there = h_all.at[(y + 2) % 4, core, rows]
        return remote(there, there, d3_send.at[n], d3_recv.at[n], at_y(way))

    def d4(step, whose):
        there = h_all.at[wrap_y[step], whose]
        return remote(there, there, d4_send.at[step], d4_recv.at[step], partner)

    start(d3_out(1))
    start(d3_out(-1))
    start(d4(0, core))
    d3_in(1).wait_recv()
    start(d3_pass(1))
    d3_in(-1).wait_recv()
    start(d3_pass(-1))
    start(d4(3, core))
    start(d4(1, core))
    d3_far(1).wait_recv()
    d3_far(-1).wait_recv()
    start(d4(2, core))
    for step in range(4):
        d4(step, 1 - core).wait_recv()

    acts = [h_all[i].reshape(rows_n, 384) for i in range(4)]
    hidden_all = jnp.concatenate([a[:, :128] for a in acts], axis=1)
    gate_grad_all = jnp.concatenate([a[:, 128:256] for a in acts], axis=1)
    up_grad_all = jnp.concatenate([a[:, 256:] for a in acts], axis=1)
    hid_buf[...] = hidden_all
    hid_copy = pltpu.make_async_copy(hid_buf, hid_hbm, out_sem.at[1])
    hid_copy.start()
    out_rows = dot(hidden_all, wd[...])
    grad_rows = dot(gate_grad_all, wg[...], ((1,), (1,))) + dot(
        up_grad_all, wu[...], ((1,), (1,))
    )
    for i in range(4):
        cols = slice(i * feat, (i + 1) * feat)
        f_mine[i] = jnp.concatenate([out_rows[:, cols], grad_rows[:, cols]], axis=1)

    mine_chunk = plane // 2
    chunks = (1 - mine_chunk, mine_chunk)

    def f(c, n, way):
        return remote(f_src.at[c, n], f_dst.at[c, n], f_send.at[c, n], f_recv.at[c, n], at_x(way))

    def f_part(c, step, lo, n):
        first = pl.multiple_of(chunks[c] * half + lo, 16)
        return f_mine[(x + step) % xs, pl.ds(first, n), :]

    for c in (0, 1):
        f_src[c, 0] = f_part(c, 2, 0, quarter).astype(BF16)
        start(f(c, 0, 1))
        f_src[c, 1] = f_part(c, 2, quarter, quarter).astype(BF16)
        start(f(c, 1, -1))
    for c in (0, 1):
        f_src[c, 2] = f_part(c, 1, quarter, quarter).astype(BF16)
        start(f(c, 2, 1))
        f_src[c, 3] = f_part(c, 3, 0, quarter).astype(BF16)
        start(f(c, 3, -1))
    for c in (0, 1):
        f(c, 0, 1).wait_recv()
        f_src[c, 4] = (f_part(c, 1, 0, quarter) + f_dst[c, 0].astype(F32)).astype(BF16)
        start(f(c, 4, 1))
        f(c, 1, -1).wait_recv()
        f_src[c, 5] = (f_part(c, 3, quarter, quarter) + f_dst[c, 1].astype(F32)).astype(BF16)
        start(f(c, 5, -1))

    def zc(j):
        return remote(z_src.at[j - 1], z_dst.at[j - 1], z_send.at[j - 1], z_recv.at[j - 1], at_plane(order[j]))

    for c in (0, 1):
        for n, way in ((2, 1), (3, -1), (4, 1), (5, -1)):
            f(c, n, way).wait_recv()
        top_sum = f_part(c, 0, 0, quarter) + f_dst[c, 4].astype(F32) + f_dst[c, 3].astype(F32)
        low_sum = f_part(c, 0, quarter, quarter) + f_dst[c, 2].astype(F32) + f_dst[c, 5].astype(F32)
        odd = plane % 2
        if c == 0:
            z_sum[0] = top_sum
            z_sum[1] = low_sum
            for j, at in ((2, odd), (3, 1 - odd)):
                z_src[j - 1] = z_sum[at].astype(BF16)
                start(zc(j))
        else:
            z_sum[2] = top_sum
            z_sum[3] = low_sum
            z_src[0] = z_sum[3 - odd].astype(BF16)
            start(zc(1))
    routes = z_sum[2 + odd]
    for j in (2, 3, 1):
        zc(j).wait_recv()
        routes = routes + z_dst[j - 1].astype(F32)

    wide = dot(squeeze((slots_n, cap_rows), 0), routes.astype(BF16))
    g_src[...] = wide.reshape(EXPERTS, SLOT, 2 * feat).astype(BF16)

    def gc(k, way):
        return remote(
            g_src.at[PLACE[k]], home_hbm.at[k], g_send.at[k - 1], g_recv.at[k - 1], at_group(way * k)
        )

    for k in (4, 3, 5, 2, 6, 1, 7):
        start(gc(k, -1))
    own_copy = pltpu.make_async_copy(g_src.at[0], home_hbm.at[0], out_sem.at[2])
    own_copy.start()
    dy_copy.wait()
    hid_copy.wait()
    own_copy.wait()
    for copy in sent:
        copy.wait_send()
    for k in range(1, 8):
        gc(k, 1).wait_recv()


def finish(home_ref, slots_ref, hid_ref, dy_ref, out_ref, grad_ref, down_hbm, down_buf, sem):
    rows, units = hid_ref.shape
    feat = out_ref.shape[1]
    step = units // 4
    copies = []
    for i in range(4):
        own = pl.ds(i * step, step)
        down_buf[own, :] = dot(hid_ref[:, own], dy_ref[...], ((0,), (0,))).astype(BF16)
        copies.append(pltpu.make_async_copy(down_buf.at[own, :], down_hbm.at[own, :], sem.at[i]))
        copies[-1].start()
    home = home_ref[...].reshape(EXPERTS * SLOT, 2 * feat).astype(F32)
    high = lax.Precision.HIGHEST
    out_ref[...] = dot(slots_ref[0], home[:, :feat], ((0,), (0,)), high).astype(BF16)
    grad_ref[...] = dot(slots_ref[1], home[:, feat:], ((0,), (0,)), high).astype(BF16)
    for copy in copies:
        copy.wait()


def per_device(tokens, cotangent, expert_ids, gate_weights, w_gate, w_up, w_down):
    tok_rows, feat = tokens.shape
    wide, units = w_gate.shape
    planes = lax.axis_size("expert") // EXPERTS
    cap_rows = EXPERTS * CAP
    rows = planes * cap_rows
    half, quarter = rows // 2, rows // 4
    vmem = pl.BlockSpec(memory_space=pltpu.VMEM)
    hbm = pl.BlockSpec(memory_space=pl.ANY)
    dma = pltpu.SemaphoreType.DMA
    block = (EXPERTS, SLOT, 2 * feat)
    part = cap_rows // 2
    home, slots, hidden, dy_rows = pl.pallas_call(
        kernel,
        out_shape=(
            jax.ShapeDtypeStruct(block, BF16),
            jax.ShapeDtypeStruct((2, EXPERTS * SLOT, tok_rows), F32),
            jax.ShapeDtypeStruct((rows, units), BF16),
            jax.ShapeDtypeStruct((rows, wide), BF16),
        ),
        in_specs=[hbm] * 7,
        out_specs=(hbm, vmem, hbm, hbm),
        scratch_shapes=[
            pltpu.VMEM((2, tok_rows), jnp.int32), pltpu.VMEM((2, tok_rows), F32),
            pltpu.VMEM((tok_rows, feat), BF16), pltpu.VMEM((tok_rows, feat), BF16), dma((4,)),
            pltpu.VMEM((wide, units), BF16), pltpu.VMEM((wide, units), BF16),
            pltpu.VMEM((units, wide), BF16), dma((3,)),
            pltpu.VMEM(block, BF16), pltpu.VMEM((len(RELAYS),) + block[1:], BF16),
            pltpu.VMEM(block, BF16), dma((len(ARRIVALS),)), dma((len(ARRIVALS),)),
            pltpu.VMEM((4, planes, 2, part, 2 * feat), BF16),
            dma((2, 3)), dma((2, 3)), dma((2, 4, 3)), dma((2, 4, 3)),
            pltpu.VMEM((4, rows, 384), F32), pltpu.VMEM((4, half, 384), F32),
            pltpu.VMEM((4, half, 384), F32), dma((4,)), dma((4,)),
            pltpu.VMEM((6, quarter, 384), BF16), pltpu.VMEM((6, quarter, 384), BF16),
            dma((6,)), dma((6,)),
            pltpu.VMEM((4, 2, half, 384), BF16), dma((4,)), dma((4,)), dma((4,)), dma((4,)),
            pltpu.VMEM((4, rows, 2 * feat), F32), pltpu.VMEM((2, 6, quarter, 2 * feat), BF16),
            pltpu.VMEM((2, 6, quarter, 2 * feat), BF16), dma((2, 6)), dma((2, 6)),
            pltpu.VMEM((4, cap_rows, 2 * feat), F32),
            pltpu.VMEM((3, cap_rows, 2 * feat), BF16), pltpu.VMEM((3, cap_rows, 2 * feat), BF16),
            dma((3,)), dma((3,)),
            pltpu.VMEM(block, BF16), dma((7,)), dma((7,)),
            pltpu.VMEM((rows, units), BF16), pltpu.VMEM((rows, wide), BF16), dma((3,)),
        ],
        compiler_params=pltpu.CompilerParams(collective_id=0, has_side_effects=True),
    )(expert_ids.T, gate_weights.T, tokens, cotangent, w_gate, w_up, w_down)
    return pl.pallas_call(
        finish,
        out_shape=(
            jax.ShapeDtypeStruct((tok_rows, feat), BF16),
            jax.ShapeDtypeStruct((tok_rows, feat), BF16),
            jax.ShapeDtypeStruct((units, wide), BF16),
        ),
        in_specs=[vmem] * 4,
        out_specs=(vmem, vmem, hbm),
        scratch_shapes=[pltpu.VMEM((units, wide), BF16), dma((4,))],
    )(home, slots, hidden, dy_rows)


def solution(mesh):
    return jax.shard_map(
        per_device,
        mesh=mesh,
        in_specs=(
            P("expert", ("dp", "tpin", "tpout")),
            P("expert", ("dp", "tpin", "tpout")),
            P("expert", None),
            P("expert", None),
            P(("dp", "tpin"), ("expert", "tpout")),
            P(("dp", "tpin"), ("expert", "tpout")),
            P(("expert", "tpout"), ("dp", "tpin")),
        ),
        out_specs=(
            P("expert", ("dp", "tpin", "tpout")),
            P("expert", ("dp", "tpin", "tpout")),
            P(("expert", "tpout"), ("dp", "tpin")),
        ),
        check_vma=False,
    )
```

time: 102 us -> 98.6 us (0.967)
  the two profiles are of different devices: /device:TPU:8 before, /device:TPU:1 now
where the time goes in v2:
time: 98.6 us; the launch traced here: 97.1 us
  Pallas kernels  96.4 us (98%)
    pallas_call x1, Pallas kernels, per_device(): pl.pallas_call(kernel, out_shape=(jax.ShapeDtypeStruct(block, BF16), jax....  93.5 us
    pallas_call x1, Pallas kernels, per_device(): pl.pallas_call(finish, out_shape=(jax.ShapeDtypeStruct((tok_rows, feat),...  2.9 us

profile of v2, /device:TPU:1, one launch (start us, length us, event | category | flops | bytes accessed | tf_op | source)
XLA Modules:
  0.0 97.1 jit_solution(9713268156901096831)
XLA Ops:
  0.6 93.5 %shard_map.94 = (bf16[8,8,384]{2,1,0:T(8,128)(2,1)}, f32[2,64,16]{2,1,0:T(8,128)}, bf16[192,512]{1,0:T(8,128)(2,1)}, bf16[192,768]{1,0:T(8,128)(2,1)}) custom-call(s32[2,16]{1,0:T(2,128)} %bitcast.2, f32[2,16]{1,0:T(2,128)} %bitcast.3, bf16[16,192]{1,0:T(8,128)(2,1)} %tok_hbm.1, bf16[16,192]{1,0:T(8,128)(2,1)} %cot_hbm.1, bf16[768,512]{1,0:T(8,128)(2,1)} %wg_hbm.1, ...), custom_call_target="tpu_custom_call" | custom-call | tf_op jit(solution)/shard_map/pallas_call | solution.py:447
  94.2 2.9 %shard_map.95 = (bf16[16,192]{1,0:T(8,128)(2,1)}, bf16[16,192]{1,0:T(8,128)(2,1)}, bf16[512,768]{1,0:T(8,128)(2,1)}) custom-call(bf16[8,8,384]{2,1,0:T(8,128)(2,1)} %get-tuple-element.7.home_ref, f32[2,64,16]{2,1,0:T(8,128)} %get-tuple-element.8.slots_ref, bf16[192,512]{1,0:T(8,128)(2,1)} %get-tuple-element.9.hid_ref, bf16[192,768]{1,0:T(8,128)(2,1)} %get-tuple-element.10.dy_ref), custom_call_target="tpu_custom_call" | custom-call | tf_op jit(solution)/shard_map/pallas_call | solution.py:481

commit v3 on v2

--- a/solution.py
+++ b/solution.py
@@ -13,12 +13,11 @@
 F32 = jnp.float32
 BF16 = jnp.bfloat16
 
-HOPS = (0, 1, 2, 3, 4, 3, 2, 1)
-AHEAD = (0, 1, 1, 1, 0, -1, -1, -1)
+LEGS = ((), (1,), (2,), (2, 1), (0, 0), (-2, -1), (-2,), (-1,))
 FIRST = (4, 3, 5, 2, 6, 1, 7)
-RELAYS = tuple((k, h) for h in (1, 2, 3) for k in (4, 3, 5, 2, 6) if HOPS[k] > h)
+RELAYS = (4, 3, 5)
+ARRIVALS = tuple((k, h) for k in range(1, 8) for h in range(len(LEGS[k])))
 PLACE = (0, 1, 3, 5, 7, 6, 4, 2)
-ARRIVALS = tuple((k, h) for k in range(1, 8) for h in range(1, HOPS[k] + 1))
 
 
 def dot(a, b, contract=((1,), (0,)), precision=None):
@@ -29,7 +28,7 @@
 
 def kernel(
     ids_hbm, gw_hbm, tok_hbm, cot_hbm, wg_hbm, wu_hbm, wd_hbm,
-    home_hbm, slots_ref, hid_hbm, dy_hbm,
+    home_hbm, slots_hbm, hid_hbm, dy_hbm,
     ids_ref, gw_ref, tok_ref, cot_ref, in_sem,
     wg, wu, wd, w_sem,
     a_src, a_relay, a_dst, a_send, a_recv,
@@ -40,7 +39,7 @@
     f_mine, f_src, f_dst, f_send, f_recv,
     z_sum, z_src, z_dst, z_send, z_recv,
     g_src, g_send, g_recv,
-    hid_buf, dy_buf, out_sem,
+    slot_buf, hid_buf, dy_buf, out_sem,
 ):
     sent = []
 
@@ -82,8 +81,9 @@
         sent.append(copy)
 
     barrier = pltpu.get_barrier_semaphore()
-    peers = [at_group(1), at_group(-1), at_x(1), at_x(-1), at_y(1), at_y(-1), partner]
+    peers = [at_group(step) for step in (2, -2, 1, -1)] + [partner]
     peers += [at_plane(p) for p in near_planes]
+    peers += [at(step) for at in (at_x, at_y) for step in (2, 1, 3)]
     for peer in peers:
         pl.semaphore_signal(barrier, inc=1, device_id=peer, device_id_type=MESH)
     inputs = [
@@ -135,23 +135,21 @@
     a_src[...] = both.reshape(EXPERTS, SLOT, 2 * feat).astype(BF16)
     a_dst[0] = a_src[0]
 
-    slots_ref[0] = slot_weights
-    slots_ref[1] = chosen
+    slot_buf[0] = slot_weights
+    slot_buf[1] = chosen
+    slot_copy = pltpu.make_async_copy(slot_buf, slots_hbm, out_sem.at[3])
+    slot_copy.start()
 
     pl.semaphore_wait(barrier, len(peers))
 
     def a_copy(k, h):
-        src = a_src.at[k] if h == 1 else a_relay.at[RELAYS.index((k, h - 1))]
-        dst = a_dst.at[PLACE[k]] if h == HOPS[k] else a_relay.at[RELAYS.index((k, h))]
+        src = a_relay.at[RELAYS.index(k)] if h else a_src.at[k]
+        dst = a_dst.at[PLACE[k]] if h == len(LEGS[k]) - 1 else a_relay.at[RELAYS.index(k)]
         n = ARRIVALS.index((k, h))
-        step = side if k == 4 else AHEAD[k]
-        return remote(src, dst, a_send.at[n], a_recv.at[n], at_group(step))
-
-    def a_pass(hop):
-        for k, h in RELAYS:
-            if h == hop:
-                a_copy(k, h).wait_recv()
-                start(a_copy(k, h + 1))
+        return remote(src, dst, a_send.at[n], a_recv.at[n], at_group(LEGS[k][h] or 2 * side))
+
+    def a_end(k):
+        a_copy(k, len(LEGS[k]) - 1).wait_recv()
 
     cap_rows = EXPERTS * CAP
     part_rows = cap_rows // 2
@@ -167,55 +165,44 @@
         there = xg.at[x, whose, c]
         return remote(there, there, b_zsend.at[c, j - 1], b_zrecv.at[c, j - 1], at_plane(order[j]))
 
-    def bx(c, j, n, step, way):
-        there = xg.at[(x + step + xs) % xs, order[j], c]
-        return remote(there, there, b_xsend.at[c, j, n], b_xrecv.at[c, j, n], at_x(way))
+    def bx(c, j, step, whose):
+        there = xg.at[whose, order[j], c]
+        return remote(there, there, b_xsend.at[c, j, step - 1], b_xrecv.at[c, j, step - 1], at_x(step))
 
     def spread_x(c, j):
-        start(bx(c, j, 0, 0, 1))
-        start(bx(c, j, 1, 0, -1))
-
-    def relay_x(c, j):
-        n, way = (0, 1) if j < 2 else (1, -1)
-        bx(c, j, n, -way, way).wait_recv()
-        start(bx(c, j, 2, -way, way))
+        for step in (2, 1, 3):
+            start(bx(c, j, step, x))
 
     def gather_first(c):
         half_in = a_dst[4 * c : 4 * c + 4].reshape(slots_n // 2, 2 * feat)
         xg[x, plane, c] = dot(squeeze((part_rows, slots_n // 2), 1), half_in).astype(BF16)
-        for j in (1, 2, 3):
+        for j in (3, 2, 1):
             start(bz(c, j, plane))
         spread_x(c, 0)
 
     for k in FIRST:
+        start(a_copy(k, 0))
+    for k in RELAYS:
+        a_copy(k, 0).wait_recv()
         start(a_copy(k, 1))
-    a_pass(1)
-    a_pass(2)
     for k in (1, 7, 2):
-        a_copy(k, HOPS[k]).wait_recv()
+        a_end(k)
     gather_first(0)
-    a_pass(3)
     for j in (1, 2, 3):
         bz(0, j, order[j]).wait_recv()
         spread_x(0, j)
-    relay_x(0, 0)
     for k in (6, 3, 5, 4):
-        a_copy(k, HOPS[k]).wait_recv()
+        a_end(k)
     gather_first(1)
-    for j in (1, 2, 3):
-        relay_x(0, j)
     for j in (1, 2, 3):
         bz(1, j, order[j]).wait_recv()
         spread_x(1, j)
-        relay_x(1, j - 1)
-    relay_x(1, 3)
     for copy in weights:
         copy.wait()
     for c in (0, 1):
         for j in range(4):
-            n, way = (1, -1) if j < 2 else (0, 1)
-            bx(c, j, n, -way, way).wait_recv()
-            bx(c, j, 2, 2, 1).wait_recv()
+            for step in (1, 2, 3):
+                bx(c, j, step, (x - step + xs) % xs).wait_recv()
 
     rows_n = planes * cap_rows
     half = rows_n // 2
@@ -245,39 +232,23 @@
         d1_src[step] = p_mine[wrap_y[step], its_rows, :]
         start(d1(step))
 
-    quarter = half // 2
-    top, bottom = pl.ds(0, quarter), pl.ds(quarter, quarter)
-
-    def d2(n, way):
-        return remote(d2_src.at[n], d2_dst.at[n], d2_send.at[n], d2_recv.at[n], at_y(way))
+
+    def d2(step):
+        return remote(
+            d2_src.at[step - 1], d2_dst.at[step - 1], d2_send.at[step - 1], d2_recv.at[step - 1], at_y(step)
+        )
 
     def pair_sum(step):
         d1(step).wait_recv()
         return p_mine[wrap_y[step], my_rows, :] + d1_dst[step]
 
-    far = pair_sum(2).astype(BF16)
-    d2_src[0] = far[:quarter]
-    start(d2(0, 1))
-    d2_src[1] = far[quarter:]
-    start(d2(1, -1))
-    ahead_sum = pair_sum(1)
-    d2_src[2] = ahead_sum[quarter:].astype(BF16)
-    start(d2(2, 1))
-    back_sum = pair_sum(3)
-    d2_src[3] = back_sum[:quarter].astype(BF16)
-    start(d2(3, -1))
-    mine = pair_sum(0)
-    d2(0, 1).wait_recv()
-    d2_src[4] = (ahead_sum[:quarter] + d2_dst[0].astype(F32)).astype(BF16)
-    start(d2(4, 1))
-    d2(1, -1).wait_recv()
-    d2_src[5] = (back_sum[quarter:] + d2_dst[1].astype(F32)).astype(BF16)
-    start(d2(5, -1))
-    for n, way in ((2, 1), (3, -1), (4, 1), (5, -1)):
-        d2(n, way).wait_recv()
-    from_back = jnp.concatenate([d2_dst[4], d2_dst[2]], axis=0).astype(F32)
-    from_ahead = jnp.concatenate([d2_dst[3], d2_dst[5]], axis=0).astype(F32)
-    total = mine + from_back + from_ahead
+    for step in (2, 1, 3):
+        d2_src[step - 1] = pair_sum(step).astype(BF16)
+        start(d2(step))
+    total = pair_sum(0)
+    for step in (1, 3, 2):
+        d2(step).wait_recv()
+        total = total + d2_dst[step - 1].astype(F32)
 
     gate, up, hidden_grad = total[:, :128], total[:, 128:256], total[:, 256:]
     sig = 1.0 / (1.0 + jnp.exp(-gate))
@@ -286,42 +257,20 @@
     up_grad = (hidden_grad * gate * sig).astype(BF16)
     h_all[y, core] = jnp.concatenate([hidden, gate_grad, up_grad], axis=1)
 
-    def d3_out(way):
-        own = h_all.at[y, core]
-        n = 0 if way == 1 else 1
-        return remote(own, own, d3_send.at[n], d3_recv.at[n], at_y(way))
-
-    def d3_in(way):
-        there = h_all.at[(y - way + 4) % 4, core]
-        n = 0 if way == 1 else 1
-        return remote(there, there, d3_send.at[n], d3_recv.at[n], at_y(way))
-
-    def d3_pass(way):
-        n, rows = (2, top) if way == 1 else (3, bottom)
-        there = h_all.at[(y - way + 4) % 4, core, rows]
-        return remote(there, there, d3_send.at[n], d3_recv.at[n], at_y(way))
-
-    def d3_far(way):
-        n, rows = (2, top) if way == 1 else (3, bottom)
-        there = h_all.at[(y + 2) % 4, core, rows]
-        return remote(there, there, d3_send.at[n], d3_recv.at[n], at_y(way))
+    def d3(step, whose):
+        there = h_all.at[whose, core]
+        return remote(there, there, d3_send.at[step - 1], d3_recv.at[step - 1], at_y(step))
 
     def d4(step, whose):
         there = h_all.at[wrap_y[step], whose]
         return remote(there, there, d4_send.at[step], d4_recv.at[step], partner)
 
-    start(d3_out(1))
-    start(d3_out(-1))
+    for step in (2, 1, 3):
+        start(d3(step, y))
     start(d4(0, core))
-    d3_in(1).wait_recv()
-    start(d3_pass(1))
-    d3_in(-1).wait_recv()
-    start(d3_pass(-1))
-    start(d4(3, core))
-    start(d4(1, core))
-    d3_far(1).wait_recv()
-    d3_far(-1).wait_recv()
-    start(d4(2, core))
+    for step in (1, 3, 2):
+        d3(step, wrap_y[4 - step]).wait_recv()
+        start(d4(4 - step, core))
     for step in range(4):
         d4(step, 1 - core).wait_recv()
 
@@ -343,51 +292,32 @@
     mine_chunk = plane // 2
     chunks = (1 - mine_chunk, mine_chunk)
 
-    def f(c, n, way):
-        return remote(f_src.at[c, n], f_dst.at[c, n], f_send.at[c, n], f_recv.at[c, n], at_x(way))
-
-    def f_part(c, step, lo, n):
-        first = pl.multiple_of(chunks[c] * half + lo, 16)
-        return f_mine[(x + step) % xs, pl.ds(first, n), :]
+    def f(c, step):
+        n = step - 1
+        return remote(f_src.at[c, n], f_dst.at[c, n], f_send.at[c, n], f_recv.at[c, n], at_x(step))
+
+    def f_part(c, step):
+        return f_mine[(x + step) % xs, pl.ds(pl.multiple_of(chunks[c] * half, half), half), :]
 
     for c in (0, 1):
-        f_src[c, 0] = f_part(c, 2, 0, quarter).astype(BF16)
-        start(f(c, 0, 1))
-        f_src[c, 1] = f_part(c, 2, quarter, quarter).astype(BF16)
-        start(f(c, 1, -1))
-    for c in (0, 1):
-        f_src[c, 2] = f_part(c, 1, quarter, quarter).astype(BF16)
-        start(f(c, 2, 1))
-        f_src[c, 3] = f_part(c, 3, 0, quarter).astype(BF16)
-        start(f(c, 3, -1))
-    for c in (0, 1):
-        f(c, 0, 1).wait_recv()
-        f_src[c, 4] = (f_part(c, 1, 0, quarter) + f_dst[c, 0].astype(F32)).astype(BF16)
-        start(f(c, 4, 1))
-        f(c, 1, -1).wait_recv()
-        f_src[c, 5] = (f_part(c, 3, quarter, quarter) + f_dst[c, 1].astype(F32)).astype(BF16)
-        start(f(c, 5, -1))
+        for step in (2, 1, 3):
+            f_src[c, step - 1] = f_part(c, step).astype(BF16)
+            start(f(c, step))
 
     def zc(j):
         return remote(z_src.at[j - 1], z_dst.at[j - 1], z_send.at[j - 1], z_recv.at[j - 1], at_plane(order[j]))
 
+    odd = plane % 2
     for c in (0, 1):
-        for n, way in ((2, 1), (3, -1), (4, 1), (5, -1)):
-            f(c, n, way).wait_recv()
-        top_sum = f_part(c, 0, 0, quarter) + f_dst[c, 4].astype(F32) + f_dst[c, 3].astype(F32)
-        low_sum = f_part(c, 0, quarter, quarter) + f_dst[c, 2].astype(F32) + f_dst[c, 5].astype(F32)
-        odd = plane % 2
-        if c == 0:
-            z_sum[0] = top_sum
-            z_sum[1] = low_sum
-            for j, at in ((2, odd), (3, 1 - odd)):
-                z_src[j - 1] = z_sum[at].astype(BF16)
-                start(zc(j))
-        else:
-            z_sum[2] = top_sum
-            z_sum[3] = low_sum
-            z_src[0] = z_sum[3 - odd].astype(BF16)
-            start(zc(1))
+        chunk_sum = f_part(c, 0)
+        for step in (1, 3, 2):
+            f(c, step).wait_recv()
+            chunk_sum = chunk_sum + f_dst[c, step - 1].astype(F32)
+        z_sum[2 * c] = chunk_sum[:cap_rows]
+        z_sum[2 * c + 1] = chunk_sum[cap_rows:]
+        for j, at in ((3, 1 - odd), (2, odd)) if c == 0 else ((1, 3 - odd),):
+            z_src[j - 1] = z_sum[at].astype(BF16)
+            start(zc(j))
     routes = z_sum[2 + odd]
     for j in (2, 3, 1):
         zc(j).wait_recv()
@@ -408,26 +338,48 @@
     dy_copy.wait()
     hid_copy.wait()
     own_copy.wait()
+    slot_copy.wait()
     for copy in sent:
         copy.wait_send()
     for k in range(1, 8):
         gc(k, 1).wait_recv()
 
 
-def finish(home_ref, slots_ref, hid_ref, dy_ref, out_ref, grad_ref, down_hbm, down_buf, sem):
+def finish(
+    home_hbm, slots_hbm, hid_hbm, dy_hbm, out_hbm, grad_hbm, down_hbm,
+    home_ref, slots_ref, hid_ref, dy_ref, out_ref, grad_ref, down_buf, in_sem, sem,
+):
     rows, units = hid_ref.shape
     feat = out_ref.shape[1]
     step = units // 4
+    inputs = [
+        pltpu.make_async_copy(src, dst, in_sem.at[i])
+        for i, (src, dst) in enumerate(
+            ((hid_hbm, hid_ref), (dy_hbm, dy_ref), (home_hbm, home_ref), (slots_hbm, slots_ref))
+        )
+    ]
+    for copy in inputs:
+        copy.start()
     copies = []
+
+    def put(src, dst):
+        copies.append(pltpu.make_async_copy(src, dst, sem.at[len(copies)]))
+        copies[-1].start()
+
+    inputs[0].wait()
+    inputs[1].wait()
     for i in range(4):
         own = pl.ds(i * step, step)
         down_buf[own, :] = dot(hid_ref[:, own], dy_ref[...], ((0,), (0,))).astype(BF16)
-        copies.append(pltpu.make_async_copy(down_buf.at[own, :], down_hbm.at[own, :], sem.at[i]))
-        copies[-1].start()
+        put(down_buf.at[own, :], down_hbm.at[own, :])
+    inputs[2].wait()
+    inputs[3].wait()
     home = home_ref[...].reshape(EXPERTS * SLOT, 2 * feat).astype(F32)
     high = lax.Precision.HIGHEST
     out_ref[...] = dot(slots_ref[0], home[:, :feat], ((0,), (0,)), high).astype(BF16)
+    put(out_ref, out_hbm)
     grad_ref[...] = dot(slots_ref[1], home[:, feat:], ((0,), (0,)), high).astype(BF16)
+    put(grad_ref, grad_hbm)
     for copy in copies:
         copy.wait()
 
@@ -438,8 +390,7 @@
     planes = lax.axis_size("expert") // EXPERTS
     cap_rows = EXPERTS * CAP
     rows = planes * cap_rows
-    half, quarter = rows // 2, rows // 4
-    vmem = pl.BlockSpec(memory_space=pltpu.VMEM)
+    half = rows // 2
     hbm = pl.BlockSpec(memory_space=pl.ANY)
     dma = pltpu.SemaphoreType.DMA
     block = (EXPERTS, SLOT, 2 * feat)
@@ -453,7 +404,7 @@
             jax.ShapeDtypeStruct((rows, wide), BF16),
         ),
         in_specs=[hbm] * 7,
-        out_specs=(hbm, vmem, hbm, hbm),
+        out_specs=(hbm, hbm, hbm, hbm),
         scratch_shapes=[
             pltpu.VMEM((2, tok_rows), jnp.int32), pltpu.VMEM((2, tok_rows), F32),
             pltpu.VMEM((tok_rows, feat), BF16), pltpu.VMEM((tok_rows, feat), BF16), dma((4,)),
@@ -465,16 +416,17 @@
             dma((2, 3)), dma((2, 3)), dma((2, 4, 3)), dma((2, 4, 3)),
             pltpu.VMEM((4, rows, 384), F32), pltpu.VMEM((4, half, 384), F32),
             pltpu.VMEM((4, half, 384), F32), dma((4,)), dma((4,)),
-            pltpu.VMEM((6, quarter, 384), BF16), pltpu.VMEM((6, quarter, 384), BF16),
-            dma((6,)), dma((6,)),
-            pltpu.VMEM((4, 2, half, 384), BF16), dma((4,)), dma((4,)), dma((4,)), dma((4,)),
-            pltpu.VMEM((4, rows, 2 * feat), F32), pltpu.VMEM((2, 6, quarter, 2 * feat), BF16),
-            pltpu.VMEM((2, 6, quarter, 2 * feat), BF16), dma((2, 6)), dma((2, 6)),
+            pltpu.VMEM((3, half, 384), BF16), pltpu.VMEM((3, half, 384), BF16),
+            dma((3,)), dma((3,)),
+            pltpu.VMEM((4, 2, half, 384), BF16), dma((3,)), dma((3,)), dma((4,)), dma((4,)),
+            pltpu.VMEM((4, rows, 2 * feat), F32), pltpu.VMEM((2, 3, half, 2 * feat), BF16),
+            pltpu.VMEM((2, 3, half, 2 * feat), BF16), dma((2, 3)), dma((2, 3)),
             pltpu.VMEM((4, cap_rows, 2 * feat), F32),
             pltpu.VMEM((3, cap_rows, 2 * feat), BF16), pltpu.VMEM((3, cap_rows, 2 * feat), BF16),
             dma((3,)), dma((3,)),
             pltpu.VMEM(block, BF16), dma((7,)), dma((7,)),
-            pltpu.VMEM((rows, units), BF16), pltpu.VMEM((rows, wide), BF16), dma((3,)),
+            pltpu.VMEM((2, EXPERTS * SLOT, tok_rows), F32),
+            pltpu.VMEM((rows, units), BF16), pltpu.VMEM((rows, wide), BF16), dma((4,)),
         ],
         compiler_params=pltpu.CompilerParams(collective_id=0, has_side_effects=True),
     )(expert_ids.T, gate_weights.T, tokens, cotangent, w_gate, w_up, w_down)
@@ -485,9 +437,14 @@
             jax.ShapeDtypeStruct((tok_rows, feat), BF16),
             jax.ShapeDtypeStruct((units, wide), BF16),
         ),
-        in_specs=[vmem] * 4,
-        out_specs=(vmem, vmem, hbm),
-        scratch_shapes=[pltpu.VMEM((units, wide), BF16), dma((4,))],
+        in_specs=[hbm] * 4,
+        out_specs=(hbm, hbm, hbm),
+        scratch_shapes=[
+            pltpu.VMEM(block, BF16), pltpu.VMEM((2, EXPERTS * SLOT, tok_rows), F32),
+            pltpu.VMEM((rows, units), BF16), pltpu.VMEM((rows, wide), BF16),
+            pltpu.VMEM((tok_rows, feat), BF16), pltpu.VMEM((tok_rows, feat), BF16),
+            pltpu.VMEM((units, wide), BF16), dma((4,)), dma((6,)),
+        ],
     )(home, slots, hidden, dy_rows)
 
 

time: 98.6 us -> 88.9 us (0.902); the launches traced: 97.1 us -> 88.8 us
  Pallas kernels: 96.4 us -> 88.1 us
    pallas_call x1, Pallas kernels: 93.5 us -> 85.7 us  [per_device(): pl.pallas_call(kernel, out_shape=(jax.ShapeDtypeStruct(block, BF16), jax....]
where the time goes in v3:
time: 88.9 us; the launch traced here: 88.8 us
  Pallas kernels  88.1 us (99%)
    pallas_call x1, Pallas kernels, per_device(): pl.pallas_call(kernel, out_shape=(jax.ShapeDtypeStruct(block, BF16), jax....  85.7 us
    pallas_call x1, Pallas kernels, per_device(): pl.pallas_call(finish, out_shape=(jax.ShapeDtypeStruct((tok_rows, feat),...  2.41 us

profile of v3, /device:TPU:1, one launch (start us, length us, event | category | flops | bytes accessed | tf_op | source)
XLA Modules:
  0.0 88.8 jit_solution(14162484363194672518)
XLA Ops:
  0.6 85.7 %shard_map.94 = (bf16[8,8,384]{2,1,0:T(8,128)(2,1)}, f32[2,64,16]{2,1,0:T(8,128)}, bf16[192,512]{1,0:T(8,128)(2,1)}, bf16[192,768]{1,0:T(8,128)(2,1)}) custom-call(s32[2,16]{1,0:T(2,128)} %bitcast.2, f32[2,16]{1,0:T(2,128)} %bitcast.3, bf16[16,192]{1,0:T(8,128)(2,1)} %tok_hbm.1, bf16[16,192]{1,0:T(8,128)(2,1)} %cot_hbm.1, bf16[768,512]{1,0:T(8,128)(2,1)} %wg_hbm.1, ...), custom_call_target="tpu_custom_call" | custom-call | tf_op jit(solution)/shard_map/pallas_call | solution.py:398
  86.3 2.4 %shard_map.95 = (bf16[16,192]{1,0:T(8,128)(2,1)}, bf16[16,192]{1,0:T(8,128)(2,1)}, bf16[512,768]{1,0:T(8,128)(2,1)}) custom-call(bf16[8,8,384]{2,1,0:T(8,128)(2,1)} %get-tuple-element.7.home_hbm, f32[2,64,16]{2,1,0:T(8,128)} %get-tuple-element.8.slots_hbm, bf16[192,512]{1,0:T(8,128)(2,1)} %get-tuple-element.9.hid_hbm, bf16[192,768]{1,0:T(8,128)(2,1)} %get-tuple-element.10.dy_hbm), custom_call_target="tpu_custom_call" | custom-call | tf_op jit(solution)/shard_map/pallas_call | solution.py:433

commit v4 on v3

--- a/solution.py
+++ b/solution.py
@@ -33,15 +33,15 @@
     wg, wu, wd, w_sem,
     a_src, a_relay, a_dst, a_send, a_recv,
     xg, b_zsend, b_zrecv, b_xsend, b_xrecv,
-    p_mine, d1_src, d1_dst, d1_send, d1_recv,
-    d2_src, d2_dst, d2_send, d2_recv,
+    p_mine, d1_dst, d1_send, d1_recv,
+    d2_own, d2_src, d2_dst, d2_send, d2_recv,
     h_all, d3_send, d3_recv, d4_send, d4_recv,
     f_mine, f_src, f_dst, f_send, f_recv,
     z_sum, z_src, z_dst, z_send, z_recv,
     g_src, g_send, g_recv,
     slot_buf, hid_buf, dy_buf, out_sem,
 ):
-    sent = []
+    sent, kept = [], []
 
     z = lax.axis_index("expert")
     x = lax.axis_index("tpout")
@@ -79,6 +79,10 @@
     def start(copy):
         copy.start()
         sent.append(copy)
+
+    def local(src, dst, sem):
+        kept.append(pltpu.make_async_copy(src, dst, sem))
+        kept[-1].start()
 
     barrier = pltpu.get_barrier_semaphore()
     peers = [at_group(step) for step in (2, -2, 1, -1)] + [partner]
@@ -137,8 +141,7 @@
 
     slot_buf[0] = slot_weights
     slot_buf[1] = chosen
-    slot_copy = pltpu.make_async_copy(slot_buf, slots_hbm, out_sem.at[3])
-    slot_copy.start()
+    local(slot_buf, slots_hbm, out_sem.at[5])
 
     pl.semaphore_wait(barrier, len(peers))
 
@@ -162,23 +165,156 @@
     order = (plane,) + near_planes
 
     def bz(c, j, whose):
-        there = xg.at[x, whose, c]
+        there = xg.at[x, c, whose]
         return remote(there, there, b_zsend.at[c, j - 1], b_zrecv.at[c, j - 1], at_plane(order[j]))
 
     def bx(c, j, step, whose):
-        there = xg.at[whose, order[j], c]
+        there = xg.at[whose, c, order[j]]
         return remote(there, there, b_xsend.at[c, j, step - 1], b_xrecv.at[c, j, step - 1], at_x(step))
 
     def spread_x(c, j):
         for step in (2, 1, 3):
             start(bx(c, j, step, x))
 
-    def gather_first(c):
+    def gather(c):
         half_in = a_dst[4 * c : 4 * c + 4].reshape(slots_n // 2, 2 * feat)
-        xg[x, plane, c] = dot(squeeze((part_rows, slots_n // 2), 1), half_in).astype(BF16)
+        xg[x, c, plane] = dot(squeeze((part_rows, slots_n // 2), 1), half_in).astype(BF16)
         for j in (3, 2, 1):
             start(bz(c, j, plane))
         spread_x(c, 0)
+
+    def gather_x(c):
+        for j in (1, 2, 3):
+            bz(c, j, order[j]).wait_recv()
+            spread_x(c, j)
+
+    half = planes * part_rows
+    core_rows = half // 2
+    my_rows = pl.ds(pl.multiple_of(core * core_rows, core_rows), core_rows)
+    its_rows = pl.ds(pl.multiple_of((1 - core) * core_rows, core_rows), core_rows)
+    wrap_y = [(y + step) % 4 for step in range(4)]
+
+    def d1(c, i):
+        return remote(
+            p_mine.at[c, wrap_y[i], its_rows], d1_dst.at[c, i], d1_send.at[c, i], d1_recv.at[c, i], partner
+        )
+
+    def products(c):
+        for j in range(4):
+            for step in (1, 2, 3):
+                bx(c, j, step, (x - step + xs) % xs).wait_recv()
+        blocks = [xg[i, c].reshape(half, 2 * feat) for i in range(4)]
+        x_all = jnp.concatenate([b[:, :feat] for b in blocks], axis=1)
+        dy_all = jnp.concatenate([b[:, feat:] for b in blocks], axis=1)
+        parts = (
+            dot(x_all, wg[...]),
+            dot(x_all, wu[...]),
+            dot(dy_all, wd[...], ((1,), (1,))),
+        )
+        for i in range(4):
+            for n, part in enumerate(parts):
+                p_mine[c, i, :, n * 128 : (n + 1) * 128] = part[:, i * 128 : (i + 1) * 128]
+        for step in (2, 1, 3, 0):
+            start(d1(c, step))
+        rows = pl.ds(c * half, half)
+        dy_buf[rows, :] = dy_all
+        local(dy_buf.at[rows], dy_hbm.at[rows], out_sem.at[c])
+
+    def d2(c, step):
+        n = step - 1
+        return remote(d2_src.at[c, n], d2_dst.at[c, n], d2_send.at[c, n], d2_recv.at[c, n], at_y(step))
+
+    def pair_sum(c, step):
+        d1(c, step).wait_recv()
+        return p_mine[c, wrap_y[step], my_rows, :] + d1_dst[c, step]
+
+    def sum_cores(c):
+        for step in (2, 1, 3):
+            d2_src[c, step - 1] = pair_sum(c, step).astype(BF16)
+            start(d2(c, step))
+        d2_own[c] = pair_sum(c, 0)
+
+    def d3(c, step, whose):
+        there = h_all.at[c, whose, core]
+        return remote(there, there, d3_send.at[c, step - 1], d3_recv.at[c, step - 1], at_y(step))
+
+    def d4(c, step, whose):
+        there = h_all.at[c, wrap_y[step], whose]
+        return remote(there, there, d4_send.at[c, step], d4_recv.at[c, step], partner)
+
+    def activate(c):
+        total = d2_own[c]
+        for step in (1, 3, 2):
+            d2(c, step).wait_recv()
+            total = total + d2_dst[c, step - 1].astype(F32)
+        gate, up, hidden_grad = total[:, :128], total[:, 128:256], total[:, 256:]
+        sig = 1.0 / (1.0 + jnp.exp(-gate))
+        hidden = (gate * sig * up).astype(BF16)
+        gate_grad = (hidden_grad * up * sig * (1.0 + gate * (1.0 - sig))).astype(BF16)
+        up_grad = (hidden_grad * gate * sig).astype(BF16)
+        h_all[c, y, core] = jnp.concatenate([hidden, gate_grad, up_grad], axis=1)
+        for step in (2, 1, 3):
+            start(d3(c, step, y))
+        start(d4(c, 0, core))
+
+    def spread_core(c):
+        for step in (1, 3, 2):
+            d3(c, step, wrap_y[4 - step]).wait_recv()
+            start(d4(c, 4 - step, core))
+
+    def f(c, step):
+        n = step - 1
+        return remote(f_src.at[c, n], f_dst.at[c, n], f_send.at[c, n], f_recv.at[c, n], at_x(step))
+
+    def results(c):
+        for step in range(4):
+            d4(c, step, 1 - core).wait_recv()
+        acts = [h_all[c, i].reshape(half, 384) for i in range(4)]
+        hidden_all = jnp.concatenate([a[:, :128] for a in acts], axis=1)
+        gate_grad_all = jnp.concatenate([a[:, 128:256] for a in acts], axis=1)
+        up_grad_all = jnp.concatenate([a[:, 256:] for a in acts], axis=1)
+        out_rows = dot(hidden_all, wd[...])
+        grad_rows = dot(gate_grad_all, wg[...], ((1,), (1,))) + dot(
+            up_grad_all, wu[...], ((1,), (1,))
+        )
+        for i in range(4):
+            cols = slice(i * feat, (i + 1) * feat)
+            f_mine[c, i] = jnp.concatenate([out_rows[:, cols], grad_rows[:, cols]], axis=1)
+        for step in (2, 1, 3):
+            f_src[c, step - 1] = f_mine[c, (x + step) % xs].astype(BF16)
+            start(f(c, step))
+        rows = pl.ds(c * half, half)
+        hid_buf[rows, :] = hidden_all
+        local(hid_buf.at[rows], hid_hbm.at[rows], out_sem.at[2 + c])
+
+    def zc(c, j):
+        n = j - 1
+        return remote(z_src.at[c, n], z_dst.at[c, n], z_send.at[c, n], z_recv.at[c, n], at_plane(order[j]))
+
+    def sum_x(c):
+        chunk_sum = f_mine[c, x]
+        for step in (1, 3, 2):
+            f(c, step).wait_recv()
+            chunk_sum = chunk_sum + f_dst[c, step - 1].astype(F32)
+        z_sum[c] = chunk_sum.reshape(planes, part_rows, 2 * feat)
+        for j in (3, 2, 1):
+            z_src[c, j - 1] = z_sum[c, order[j]].astype(BF16)
+            start(zc(c, j))
+
+    def gc(k, way):
+        return remote(
+            g_src.at[PLACE[k]], home_hbm.at[k], g_send.at[k - 1], g_recv.at[k - 1], at_group(way * k)
+        )
+
+    def go_home(c):
+        routes = z_sum[c, plane]
+        for j in (1, 2, 3):
+            zc(c, j).wait_recv()
+            routes = routes + z_dst[c, j - 1].astype(F32)
+        wide = dot(squeeze((slots_n // 2, part_rows), 0), routes.astype(BF16))
+        g_src[4 * c : 4 * c + 4] = wide.reshape(EXPERTS // 2, SLOT, 2 * feat).astype(BF16)
+        for k in (4, 3, 5, 6) if c else (2, 1, 7):
+            start(gc(k, -1))
 
     for k in FIRST:
         start(a_copy(k, 0))
@@ -187,158 +323,31 @@
         start(a_copy(k, 1))
     for k in (1, 7, 2):
         a_end(k)
-    gather_first(0)
-    for j in (1, 2, 3):
-        bz(0, j, order[j]).wait_recv()
-        spread_x(0, j)
+    gather(0)
+    gather_x(0)
     for k in (6, 3, 5, 4):
         a_end(k)
-    gather_first(1)
-    for j in (1, 2, 3):
-        bz(1, j, order[j]).wait_recv()
-        spread_x(1, j)
+    gather(1)
     for copy in weights:
         copy.wait()
-    for c in (0, 1):
-        for j in range(4):
-            for step in (1, 2, 3):
-                bx(c, j, step, (x - step + xs) % xs).wait_recv()
-
-    rows_n = planes * cap_rows
-    half = rows_n // 2
-    blocks = [xg[i].reshape(rows_n, 2 * feat) for i in range(4)]
-    x_all = jnp.concatenate([b[:, :feat] for b in blocks], axis=1)
-    dy_all = jnp.concatenate([b[:, feat:] for b in blocks], axis=1)
-    dy_buf[...] = dy_all
-    dy_copy = pltpu.make_async_copy(dy_buf, dy_hbm, out_sem.at[0])
-    dy_copy.start()
-    parts = (
-        dot(x_all, wg[...]),
-        dot(x_all, wu[...]),
-        dot(dy_all, wd[...], ((1,), (1,))),
-    )
-    for i in range(4):
-        for n, part in enumerate(parts):
-            p_mine[i, :, n * 128 : (n + 1) * 128] = part[:, i * 128 : (i + 1) * 128]
-
-    my_rows = pl.ds(pl.multiple_of(core * half, half), half)
-    its_rows = pl.ds(pl.multiple_of((1 - core) * half, half), half)
-
-    def d1(i):
-        return remote(d1_src.at[i], d1_dst.at[i], d1_send.at[i], d1_recv.at[i], partner)
-
-    wrap_y = [(y + step) % 4 for step in range(4)]
-    for step in (2, 1, 3, 0):
-        d1_src[step] = p_mine[wrap_y[step], its_rows, :]
-        start(d1(step))
-
-
-    def d2(step):
-        return remote(
-            d2_src.at[step - 1], d2_dst.at[step - 1], d2_send.at[step - 1], d2_recv.at[step - 1], at_y(step)
-        )
-
-    def pair_sum(step):
-        d1(step).wait_recv()
-        return p_mine[wrap_y[step], my_rows, :] + d1_dst[step]
-
-    for step in (2, 1, 3):
-        d2_src[step - 1] = pair_sum(step).astype(BF16)
-        start(d2(step))
-    total = pair_sum(0)
-    for step in (1, 3, 2):
-        d2(step).wait_recv()
-        total = total + d2_dst[step - 1].astype(F32)
-
-    gate, up, hidden_grad = total[:, :128], total[:, 128:256], total[:, 256:]
-    sig = 1.0 / (1.0 + jnp.exp(-gate))
-    hidden = (gate * sig * up).astype(BF16)
-    gate_grad = (hidden_grad * up * sig * (1.0 + gate * (1.0 - sig))).astype(BF16)
-    up_grad = (hidden_grad * gate * sig).astype(BF16)
-    h_all[y, core] = jnp.concatenate([hidden, gate_grad, up_grad], axis=1)
-
-    def d3(step, whose):
-        there = h_all.at[whose, core]
-        return remote(there, there, d3_send.at[step - 1], d3_recv.at[step - 1], at_y(step))
-
-    def d4(step, whose):
-        there = h_all.at[wrap_y[step], whose]
-        return remote(there, there, d4_send.at[step], d4_recv.at[step], partner)
-
-    for step in (2, 1, 3):
-        start(d3(step, y))
-    start(d4(0, core))
-    for step in (1, 3, 2):
-        d3(step, wrap_y[4 - step]).wait_recv()
-        start(d4(4 - step, core))
-    for step in range(4):
-        d4(step, 1 - core).wait_recv()
-
-    acts = [h_all[i].reshape(rows_n, 384) for i in range(4)]
-    hidden_all = jnp.concatenate([a[:, :128] for a in acts], axis=1)
-    gate_grad_all = jnp.concatenate([a[:, 128:256] for a in acts], axis=1)
-    up_grad_all = jnp.concatenate([a[:, 256:] for a in acts], axis=1)
-    hid_buf[...] = hidden_all
-    hid_copy = pltpu.make_async_copy(hid_buf, hid_hbm, out_sem.at[1])
-    hid_copy.start()
-    out_rows = dot(hidden_all, wd[...])
-    grad_rows = dot(gate_grad_all, wg[...], ((1,), (1,))) + dot(
-        up_grad_all, wu[...], ((1,), (1,))
-    )
-    for i in range(4):
-        cols = slice(i * feat, (i + 1) * feat)
-        f_mine[i] = jnp.concatenate([out_rows[:, cols], grad_rows[:, cols]], axis=1)
-
-    mine_chunk = plane // 2
-    chunks = (1 - mine_chunk, mine_chunk)
-
-    def f(c, step):
-        n = step - 1
-        return remote(f_src.at[c, n], f_dst.at[c, n], f_send.at[c, n], f_recv.at[c, n], at_x(step))
-
-    def f_part(c, step):
-        return f_mine[(x + step) % xs, pl.ds(pl.multiple_of(chunks[c] * half, half), half), :]
-
-    for c in (0, 1):
-        for step in (2, 1, 3):
-            f_src[c, step - 1] = f_part(c, step).astype(BF16)
-            start(f(c, step))
-
-    def zc(j):
-        return remote(z_src.at[j - 1], z_dst.at[j - 1], z_send.at[j - 1], z_recv.at[j - 1], at_plane(order[j]))
-
-    odd = plane % 2
-    for c in (0, 1):
-        chunk_sum = f_part(c, 0)
-        for step in (1, 3, 2):
-            f(c, step).wait_recv()
-            chunk_sum = chunk_sum + f_dst[c, step - 1].astype(F32)
-        z_sum[2 * c] = chunk_sum[:cap_rows]
-        z_sum[2 * c + 1] = chunk_sum[cap_rows:]
-        for j, at in ((3, 1 - odd), (2, odd)) if c == 0 else ((1, 3 - odd),):
-            z_src[j - 1] = z_sum[at].astype(BF16)
-            start(zc(j))
-    routes = z_sum[2 + odd]
-    for j in (2, 3, 1):
-        zc(j).wait_recv()
-        routes = routes + z_dst[j - 1].astype(F32)
-
-    wide = dot(squeeze((slots_n, cap_rows), 0), routes.astype(BF16))
-    g_src[...] = wide.reshape(EXPERTS, SLOT, 2 * feat).astype(BF16)
-
-    def gc(k, way):
-        return remote(
-            g_src.at[PLACE[k]], home_hbm.at[k], g_send.at[k - 1], g_recv.at[k - 1], at_group(way * k)
-        )
-
-    for k in (4, 3, 5, 2, 6, 1, 7):
-        start(gc(k, -1))
-    own_copy = pltpu.make_async_copy(g_src.at[0], home_hbm.at[0], out_sem.at[2])
-    own_copy.start()
-    dy_copy.wait()
-    hid_copy.wait()
-    own_copy.wait()
-    slot_copy.wait()
+    products(0)
+    sum_cores(0)
+    gather_x(1)
+    activate(0)
+    products(1)
+    sum_cores(1)
+    spread_core(0)
+    results(0)
+    activate(1)
+    sum_x(0)
+    spread_core(1)
+    results(1)
+    go_home(0)
+    local(g_src.at[0], home_hbm.at[0], out_sem.at[4])
+    sum_x(1)
+    go_home(1)
+    for copy in kept:
+        copy.wait()
     for copy in sent:
         copy.wait_send()
     for k in range(1, 8):
@@ -412,21 +421,21 @@
             pltpu.VMEM((units, wide), BF16), dma((3,)),
             pltpu.VMEM(block, BF16), pltpu.VMEM((len(RELAYS),) + block[1:], BF16),
             pltpu.VMEM(block, BF16), dma((len(ARRIVALS),)), dma((len(ARRIVALS),)),
-            pltpu.VMEM((4, planes, 2, part, 2 * feat), BF16),
+            pltpu.VMEM((4, 2, planes, part, 2 * feat), BF16),
             dma((2, 3)), dma((2, 3)), dma((2, 4, 3)), dma((2, 4, 3)),
-            pltpu.VMEM((4, rows, 384), F32), pltpu.VMEM((4, half, 384), F32),
-            pltpu.VMEM((4, half, 384), F32), dma((4,)), dma((4,)),
-            pltpu.VMEM((3, half, 384), BF16), pltpu.VMEM((3, half, 384), BF16),
-            dma((3,)), dma((3,)),
-            pltpu.VMEM((4, 2, half, 384), BF16), dma((3,)), dma((3,)), dma((4,)), dma((4,)),
-            pltpu.VMEM((4, rows, 2 * feat), F32), pltpu.VMEM((2, 3, half, 2 * feat), BF16),
+            pltpu.VMEM((2, 4, half, 384), F32), pltpu.VMEM((2, 4, half // 2, 384), F32), dma((2, 4)), dma((2, 4)),
+            pltpu.VMEM((2, half // 2, 384), F32),
+            pltpu.VMEM((2, 3, half // 2, 384), BF16), pltpu.VMEM((2, 3, half // 2, 384), BF16),
+            dma((2, 3)), dma((2, 3)),
+            pltpu.VMEM((2, 4, 2, half // 2, 384), BF16), dma((2, 3)), dma((2, 3)), dma((2, 4)), dma((2, 4)),
+            pltpu.VMEM((2, 4, half, 2 * feat), F32), pltpu.VMEM((2, 3, half, 2 * feat), BF16),
             pltpu.VMEM((2, 3, half, 2 * feat), BF16), dma((2, 3)), dma((2, 3)),
-            pltpu.VMEM((4, cap_rows, 2 * feat), F32),
-            pltpu.VMEM((3, cap_rows, 2 * feat), BF16), pltpu.VMEM((3, cap_rows, 2 * feat), BF16),
-            dma((3,)), dma((3,)),
+            pltpu.VMEM((2, planes, part, 2 * feat), F32),
+            pltpu.VMEM((2, 3, part, 2 * feat), BF16), pltpu.VMEM((2, 3, part, 2 * feat), BF16),
+            dma((2, 3)), dma((2, 3)),
             pltpu.VMEM(block, BF16), dma((7,)), dma((7,)),
             pltpu.VMEM((2, EXPERTS * SLOT, tok_rows), F32),
-            pltpu.VMEM((rows, units), BF16), pltpu.VMEM((rows, wide), BF16), dma((4,)),
+            pltpu.VMEM((rows, units), BF16), pltpu.VMEM((rows, wide), BF16), dma((6,)),
         ],
         compiler_params=pltpu.CompilerParams(collective_id=0, has_side_effects=True),
     )(expert_ids.T, gate_weights.T, tokens, cotangent, w_gate, w_up, w_down)

time: 88.9 us -> 87.4 us (0.983)
  Pallas kernels: 88.1 us -> 86.5 us
    pallas_call x1, Pallas kernels: 85.7 us -> 84.1 us  [per_device(): pl.pallas_call(kernel, out_shape=(jax.ShapeDtypeStruct(block, BF16), jax....]
where the time goes in v4:
time: 87.4 us; the launch traced here: 87.2 us
  Pallas kernels  86.5 us (99%)
    pallas_call x1, Pallas kernels, per_device(): pl.pallas_call(kernel, out_shape=(jax.ShapeDtypeStruct(block, BF16), jax....  84.1 us
    pallas_call x1, Pallas kernels, per_device(): pl.pallas_call(finish, out_shape=(jax.ShapeDtypeStruct((tok_rows, feat),...  2.41 us

profile of v4, /device:TPU:1, one launch (start us, length us, event | category | flops | bytes accessed | tf_op | source)
XLA Modules:
  0.0 87.2 jit_solution(18039755662552783114)
XLA Ops:
  0.6 84.1 %shard_map.94 = (bf16[8,8,384]{2,1,0:T(8,128)(2,1)}, f32[2,64,16]{2,1,0:T(8,128)}, bf16[192,512]{1,0:T(8,128)(2,1)}, bf16[192,768]{1,0:T(8,128)(2,1)}) custom-call(s32[2,16]{1,0:T(2,128)} %bitcast.2, f32[2,16]{1,0:T(2,128)} %bitcast.3, bf16[16,192]{1,0:T(8,128)(2,1)} %tok_hbm.1, bf16[16,192]{1,0:T(8,128)(2,1)} %cot_hbm.1, bf16[768,512]{1,0:T(8,128)(2,1)} %wg_hbm.1, ...), custom_call_target="tpu_custom_call" | custom-call | tf_op jit(solution)/shard_map/pallas_call | solution.py:407
  84.8 2.4 %shard_map.95 = (bf16[16,192]{1,0:T(8,128)(2,1)}, bf16[16,192]{1,0:T(8,128)(2,1)}, bf16[512,768]{1,0:T(8,128)(2,1)}) custom-call(bf16[8,8,384]{2,1,0:T(8,128)(2,1)} %get-tuple-element.7.home_hbm, f32[2,64,16]{2,1,0:T(8,128)} %get-tuple-element.8.slots_hbm, bf16[192,512]{1,0:T(8,128)(2,1)} %get-tuple-element.9.hid_hbm, bf16[192,768]{1,0:T(8,128)(2,1)} %get-tuple-element.10.dy_hbm), custom_call_target="tpu_custom_call" | custom-call | tf_op jit(solution)/shard_map/pallas_call | solution.py:442

commit v5 on v4

--- a/solution.py
+++ b/solution.py
@@ -331,21 +331,21 @@
     for copy in weights:
         copy.wait()
     products(0)
+    gather_x(1)
     sum_cores(0)
-    gather_x(1)
-    activate(0)
     products(1)
     sum_cores(1)
+    activate(0)
+    activate(1)
     spread_core(0)
+    spread_core(1)
     results(0)
-    activate(1)
+    results(1)
+    sum_x(1)
     sum_x(0)
-    spread_core(1)
-    results(1)
+    go_home(1)
     go_home(0)
     local(g_src.at[0], home_hbm.at[0], out_sem.at[4])
-    sum_x(1)
-    go_home(1)
     for copy in kept:
         copy.wait()
     for copy in sent:

time: 87.4 us -> 87.9 us (level)
  no operation moved by 1% of the time
where the time goes in v5:
time: 87.9 us; the launch traced here: 87.4 us
  Pallas kernels  86.8 us (99%)
    pallas_call x1, Pallas kernels, per_device(): pl.pallas_call(kernel, out_shape=(jax.ShapeDtypeStruct(block, BF16), jax....  84.3 us
    pallas_call x1, Pallas kernels, per_device(): pl.pallas_call(finish, out_shape=(jax.ShapeDtypeStruct((tok_rows, feat),...  2.41 us

profile of v5, /device:TPU:1, one launch (start us, length us, event | category | flops | bytes accessed | tf_op | source)
XLA Modules:
  0.0 87.4 jit_solution(11544592080278261624)
XLA Ops:
  0.6 84.3 %shard_map.94 = (bf16[8,8,384]{2,1,0:T(8,128)(2,1)}, f32[2,64,16]{2,1,0:T(8,128)}, bf16[192,512]{1,0:T(8,128)(2,1)}, bf16[192,768]{1,0:T(8,128)(2,1)}) custom-call(s32[2,16]{1,0:T(2,128)} %bitcast.2, f32[2,16]{1,0:T(2,128)} %bitcast.3, bf16[16,192]{1,0:T(8,128)(2,1)} %tok_hbm.1, bf16[16,192]{1,0:T(8,128)(2,1)} %cot_hbm.1, bf16[768,512]{1,0:T(8,128)(2,1)} %wg_hbm.1, ...), custom_call_target="tpu_custom_call" | custom-call | tf_op jit(solution)/shard_map/pallas_call | solution.py:407
  85.0 2.4 %shard_map.95 = (bf16[16,192]{1,0:T(8,128)(2,1)}, bf16[16,192]{1,0:T(8,128)(2,1)}, bf16[512,768]{1,0:T(8,128)(2,1)}) custom-call(bf16[8,8,384]{2,1,0:T(8,128)(2,1)} %get-tuple-element.7.home_hbm, f32[2,64,16]{2,1,0:T(8,128)} %get-tuple-element.8.slots_hbm, bf16[192,512]{1,0:T(8,128)(2,1)} %get-tuple-element.9.hid_hbm, bf16[192,768]{1,0:T(8,128)(2,1)} %get-tuple-element.10.dy_hbm), custom_call_target="tpu_custom_call" | custom-call | tf_op jit(solution)/shard_map/pallas_call | solution.py:442

commit v6 on v4

--- a/solution.py
+++ b/solution.py
@@ -13,10 +13,10 @@
 F32 = jnp.float32
 BF16 = jnp.bfloat16
 
-LEGS = ((), (1,), (2,), (2, 1), (0, 0), (-2, -1), (-2,), (-1,))
-FIRST = (4, 3, 5, 2, 6, 1, 7)
-RELAYS = (4, 3, 5)
-ARRIVALS = tuple((k, h) for k in range(1, 8) for h in range(len(LEGS[k])))
+HOPS = (0, 1, 2, 3, 0, 3, 2, 1)
+AHEAD = (0, 1, 1, 1, 0, -1, -1, -1)
+ARRIVALS = tuple((k, h) for k in range(1, 8) for h in range(1, HOPS[k] + 1))
+RELAYS = tuple((k, h) for h in (1, 2) for k in (3, 5, 2, 6) if HOPS[k] > h)
 PLACE = (0, 1, 3, 5, 7, 6, 4, 2)
 
 
@@ -28,10 +28,10 @@
 
 def kernel(
     ids_hbm, gw_hbm, tok_hbm, cot_hbm, wg_hbm, wu_hbm, wd_hbm,
-    home_hbm, slots_hbm, hid_hbm, dy_hbm,
+    home_hbm, slots_hbm, down_hbm,
     ids_ref, gw_ref, tok_ref, cot_ref, in_sem,
     wg, wu, wd, w_sem,
-    a_src, a_relay, a_dst, a_send, a_recv,
+    a_src, a_relay, a_dst, a_send, a_recv, far_relay, far_send, far_recv,
     xg, b_zsend, b_zrecv, b_xsend, b_xrecv,
     p_mine, d1_dst, d1_send, d1_recv,
     d2_own, d2_src, d2_dst, d2_send, d2_recv,
@@ -39,7 +39,7 @@
     f_mine, f_src, f_dst, f_send, f_recv,
     z_sum, z_src, z_dst, z_send, z_recv,
     g_src, g_send, g_recv,
-    slot_buf, hid_buf, dy_buf, out_sem,
+    slot_buf, hid_buf, dy_buf, down_buf, out_sem,
 ):
     sent, kept = [], []
 
@@ -85,11 +85,18 @@
         kept[-1].start()
 
     barrier = pltpu.get_barrier_semaphore()
-    peers = [at_group(step) for step in (2, -2, 1, -1)] + [partner]
+    far_way = 1 - 2 * ((group + 2) % EXPERTS // 4)
+    relays_far = 1 - group // 4
+    peers = [at_group(step) for step in (2 * far_way, 1, -1)] + [partner]
     peers += [at_plane(p) for p in near_planes]
     peers += [at(step) for at in (at_x, at_y) for step in (2, 1, 3)]
     for peer in peers:
         pl.semaphore_signal(barrier, inc=1, device_id=peer, device_id_type=MESH)
+
+    @pl.when(relays_far == 1)
+    def _():
+        pl.semaphore_signal(barrier, inc=1, device_id=at_group(-2 * far_way), device_id_type=MESH)
+
     inputs = [
         pltpu.make_async_copy(src, dst, in_sem.at[i])
         for i, (src, dst) in enumerate(
@@ -141,18 +148,34 @@
 
     slot_buf[0] = slot_weights
     slot_buf[1] = chosen
-    local(slot_buf, slots_hbm, out_sem.at[5])
-
-    pl.semaphore_wait(barrier, len(peers))
+    local(slot_buf, slots_hbm, out_sem.at[1])
+
+    pl.semaphore_wait(barrier, len(peers) + relays_far)
 
     def a_copy(k, h):
-        src = a_relay.at[RELAYS.index(k)] if h else a_src.at[k]
-        dst = a_dst.at[PLACE[k]] if h == len(LEGS[k]) - 1 else a_relay.at[RELAYS.index(k)]
+        src = a_src.at[k] if h == 1 else a_relay.at[RELAYS.index((k, h - 1))]
+        dst = a_dst.at[PLACE[k]] if h == HOPS[k] else a_relay.at[RELAYS.index((k, h))]
         n = ARRIVALS.index((k, h))
-        return remote(src, dst, a_send.at[n], a_recv.at[n], at_group(LEGS[k][h] or 2 * side))
+        return remote(src, dst, a_send.at[n], a_recv.at[n], at_group(AHEAD[k]))
+
+    def a_far(way):
+        n = (1 - way) // 2
+        return remote(a_src.at[4], far_relay.at[n], far_send.at[2], far_recv.at[n], at_group(2 * way))
+
+    def a_far_end(way):
+        n = (1 - way) // 2
+        return remote(
+            far_relay.at[n], a_dst.at[PLACE[4]], far_send.at[n], far_recv.at[2], at_group(2 * way)
+        )
+
+    def a_pass(hop):
+        for k, h in RELAYS:
+            if h == hop:
+                a_copy(k, h).wait_recv()
+                start(a_copy(k, h + 1))
 
     def a_end(k):
-        a_copy(k, len(LEGS[k]) - 1).wait_recv()
+        (a_copy(k, HOPS[k]) if HOPS[k] else a_far_end(1)).wait_recv()
 
     cap_rows = EXPERTS * CAP
     part_rows = cap_rows // 2
@@ -218,7 +241,6 @@
             start(d1(c, step))
         rows = pl.ds(c * half, half)
         dy_buf[rows, :] = dy_all
-        local(dy_buf.at[rows], dy_hbm.at[rows], out_sem.at[c])
 
     def d2(c, step):
         n = step - 1
@@ -285,7 +307,6 @@
             start(f(c, step))
         rows = pl.ds(c * half, half)
         hid_buf[rows, :] = hidden_all
-        local(hid_buf.at[rows], hid_hbm.at[rows], out_sem.at[2 + c])
 
     def zc(c, j):
         n = j - 1
@@ -316,11 +337,18 @@
         for k in (4, 3, 5, 6) if c else (2, 1, 7):
             start(gc(k, -1))
 
-    for k in FIRST:
-        start(a_copy(k, 0))
-    for k in RELAYS:
-        a_copy(k, 0).wait_recv()
+    start(a_far(far_way))
+    for k in (3, 5, 2, 6, 1, 7):
         start(a_copy(k, 1))
+    a_pass(1)
+
+    @pl.when(relays_far == 1)
+    def _():
+        for way in (1, -1):
+            a_far(way).wait_recv()
+            a_far_end(way).start()
+
+    a_pass(2)
     for k in (1, 7, 2):
         a_end(k)
     gather(0)
@@ -343,53 +371,56 @@
     spread_core(1)
     results(1)
     go_home(0)
-    local(g_src.at[0], home_hbm.at[0], out_sem.at[4])
+    local(g_src.at[0], home_hbm.at[0], out_sem.at[0])
     sum_x(1)
     go_home(1)
+    down_buf[...] = dot(hid_buf[...], dy_buf[...], ((0,), (0,))).astype(BF16)
+    local(down_buf, down_hbm, out_sem.at[2])
+    for copy in sent:
+        copy.wait_send()
+
+    @pl.when(relays_far == 1)
+    def _():
+        for way in (1, -1):
+            a_far_end(way).wait_send()
+
     for copy in kept:
         copy.wait()
-    for copy in sent:
-        copy.wait_send()
     for k in range(1, 8):
         gc(k, 1).wait_recv()
 
 
 def finish(
-    home_hbm, slots_hbm, hid_hbm, dy_hbm, out_hbm, grad_hbm, down_hbm,
-    home_ref, slots_ref, hid_ref, dy_ref, out_ref, grad_ref, down_buf, in_sem, sem,
+    home_hbm, slots_hbm, made_hbm, out_hbm, grad_hbm, down_hbm,
+    home_ref, slots_ref, out_ref, grad_ref, down_buf, in_sem, made_sem, sem,
 ):
-    rows, units = hid_ref.shape
     feat = out_ref.shape[1]
-    step = units // 4
+    step = down_buf.shape[0] // 4
     inputs = [
-        pltpu.make_async_copy(src, dst, in_sem.at[i])
-        for i, (src, dst) in enumerate(
-            ((hid_hbm, hid_ref), (dy_hbm, dy_ref), (home_hbm, home_ref), (slots_hbm, slots_ref))
-        )
+        pltpu.make_async_copy(home_hbm, home_ref, in_sem.at[0]),
+        pltpu.make_async_copy(slots_hbm, slots_ref, in_sem.at[1]),
     ]
-    for copy in inputs:
-        copy.start()
-    copies = []
-
-    def put(src, dst):
-        copies.append(pltpu.make_async_copy(src, dst, sem.at[len(copies)]))
-        copies[-1].start()
-
-    inputs[0].wait()
-    inputs[1].wait()
+    made, done = [], []
     for i in range(4):
         own = pl.ds(i * step, step)
-        down_buf[own, :] = dot(hid_ref[:, own], dy_ref[...], ((0,), (0,))).astype(BF16)
-        put(down_buf.at[own, :], down_hbm.at[own, :])
-    inputs[2].wait()
-    inputs[3].wait()
+        made.append(pltpu.make_async_copy(made_hbm.at[own, :], down_buf.at[own, :], made_sem.at[i]))
+        done.append(pltpu.make_async_copy(down_buf.at[own, :], down_hbm.at[own, :], sem.at[i]))
+    for copy in inputs + made:
+        copy.start()
+    for copy in inputs:
+        copy.wait()
     home = home_ref[...].reshape(EXPERTS * SLOT, 2 * feat).astype(F32)
     high = lax.Precision.HIGHEST
+    for came, goes in zip(made, done):
+        came.wait()
+        goes.start()
     out_ref[...] = dot(slots_ref[0], home[:, :feat], ((0,), (0,)), high).astype(BF16)
-    put(out_ref, out_hbm)
+    done.append(pltpu.make_async_copy(out_ref, out_hbm, sem.at[4]))
+    done[-1].start()
     grad_ref[...] = dot(slots_ref[1], home[:, feat:], ((0,), (0,)), high).astype(BF16)
-    put(grad_ref, grad_hbm)
-    for copy in copies:
+    done.append(pltpu.make_async_copy(grad_ref, grad_hbm, sem.at[5]))
+    done[-1].start()
+    for copy in done:
         copy.wait()
 
 
@@ -404,16 +435,15 @@
     dma = pltpu.SemaphoreType.DMA
     block = (EXPERTS, SLOT, 2 * feat)
     part = cap_rows // 2
-    home, slots, hidden, dy_rows = pl.pallas_call(
+    home, slots, made = pl.pallas_call(
         kernel,
         out_shape=(
             jax.ShapeDtypeStruct(block, BF16),
             jax.ShapeDtypeStruct((2, EXPERTS * SLOT, tok_rows), F32),
-            jax.ShapeDtypeStruct((rows, units), BF16),
-            jax.ShapeDtypeStruct((rows, wide), BF16),
+            jax.ShapeDtypeStruct((units, wide), BF16),
         ),
         in_specs=[hbm] * 7,
-        out_specs=(hbm, hbm, hbm, hbm),
+        out_specs=(hbm, hbm, hbm),
         scratch_shapes=[
             pltpu.VMEM((2, tok_rows), jnp.int32), pltpu.VMEM((2, tok_rows), F32),
             pltpu.VMEM((tok_rows, feat), BF16), pltpu.VMEM((tok_rows, feat), BF16), dma((4,)),
@@ -421,6 +451,7 @@
             pltpu.VMEM((units, wide), BF16), dma((3,)),
             pltpu.VMEM(block, BF16), pltpu.VMEM((len(RELAYS),) + block[1:], BF16),
             pltpu.VMEM(block, BF16), dma((len(ARRIVALS),)), dma((len(ARRIVALS),)),
+            pltpu.VMEM((2,) + block[1:], BF16), dma((3,)), dma((3,)),
             pltpu.VMEM((4, 2, planes, part, 2 * feat), BF16),
             dma((2, 3)), dma((2, 3)), dma((2, 4, 3)), dma((2, 4, 3)),
             pltpu.VMEM((2, 4, half, 384), F32), pltpu.VMEM((2, 4, half // 2, 384), F32), dma((2, 4)), dma((2, 4)),
@@ -435,7 +466,8 @@
             dma((2, 3)), dma((2, 3)),
             pltpu.VMEM(block, BF16), dma((7,)), dma((7,)),
             pltpu.VMEM((2, EXPERTS * SLOT, tok_rows), F32),
-            pltpu.VMEM((rows, units), BF16), pltpu.VMEM((rows, wide), BF16), dma((6,)),
+            pltpu.VMEM((rows, units), BF16), pltpu.VMEM((rows, wide), BF16),
+            pltpu.VMEM((units, wide), BF16), dma((3,)),
         ],
         compiler_params=pltpu.CompilerParams(collective_id=0, has_side_effects=True),
     )(expert_ids.T, gate_weights.T, tokens, cotangent, w_gate, w_up, w_down)
@@ -446,15 +478,14 @@
             jax.ShapeDtypeStruct((tok_rows, feat), BF16),
             jax.ShapeDtypeStruct((units, wide), BF16),
         ),
-        in_specs=[hbm] * 4,
+        in_specs=[hbm] * 3,
         out_specs=(hbm, hbm, hbm),
         scratch_shapes=[
             pltpu.VMEM(block, BF16), pltpu.VMEM((2, EXPERTS * SLOT, tok_rows), F32),
-            pltpu.VMEM((rows, units), BF16), pltpu.VMEM((rows, wide), BF16),
             pltpu.VMEM((tok_rows, feat), BF16), pltpu.VMEM((tok_rows, feat), BF16),
-            pltpu.VMEM((units, wide), BF16), dma((4,)), dma((6,)),
+            pltpu.VMEM((units, wide), BF16), dma((2,)), dma((4,)), dma((6,)),
         ],
-    )(home, slots, hidden, dy_rows)
+    )(home, slots, made)
 
 
 def solution(mesh):

time: 87.4 us -> 87.9 us (level)
  no operation moved by 1% of the time
where the time goes in v6:
time: 87.9 us; the launch traced here: 87.7 us
  Pallas kernels  87.1 us (99%)
    pallas_call x1, Pallas kernels, per_device(): pl.pallas_call(kernel, out_shape=(jax.ShapeDtypeStruct(block, BF16), jax....  84.8 us
    pallas_call x1, Pallas kernels, per_device(): pl.pallas_call(finish, out_shape=(jax.ShapeDtypeStruct((tok_rows, feat),...  2.23 us

profile of v6, /device:TPU:1, one launch (start us, length us, event | category | flops | bytes accessed | tf_op | source)
XLA Modules:
  0.0 87.7 jit_solution(15713251214404220411)
XLA Ops:
  0.6 84.8 %shard_map.94 = (bf16[8,8,384]{2,1,0:T(8,128)(2,1)}, f32[2,64,16]{2,1,0:T(8,128)}, bf16[512,768]{1,0:T(8,128)(2,1)}) custom-call(s32[2,16]{1,0:T(2,128)} %bitcast.2, f32[2,16]{1,0:T(2,128)} %bitcast.3, bf16[16,192]{1,0:T(8,128)(2,1)} %tok_hbm.1, bf16[16,192]{1,0:T(8,128)(2,1)} %cot_hbm.1, bf16[768,512]{1,0:T(8,128)(2,1)} %wg_hbm.1, bf16[768,512]{1,0:T(8,128)(2,1)} %wu_hbm.1, ...), custom_call_target="tpu_custom_call" | custom-call | tf_op jit(solution)/shard_map/pallas_call | solution.py:438
  85.5 2.2 %shard_map.95 = (bf16[16,192]{1,0:T(8,128)(2,1)}, bf16[16,192]{1,0:T(8,128)(2,1)}, bf16[512,768]{1,0:T(8,128)(2,1)}) custom-call(bf16[8,8,384]{2,1,0:T(8,128)(2,1)} %get-tuple-element.6.home_hbm, f32[2,64,16]{2,1,0:T(8,128)} %get-tuple-element.7.slots_hbm, bf16[512,768]{1,0:T(8,128)(2,1)} %get-tuple-element.8.made_hbm), custom_call_target="tpu_custom_call" | custom-call | tf_op jit(solution)/shard_map/pallas_call | solution.py:474

commit v7 on v6

--- a/solution.py
+++ b/solution.py
@@ -13,10 +13,10 @@
 F32 = jnp.float32
 BF16 = jnp.bfloat16
 
-HOPS = (0, 1, 2, 3, 0, 3, 2, 1)
-AHEAD = (0, 1, 1, 1, 0, -1, -1, -1)
-ARRIVALS = tuple((k, h) for k in range(1, 8) for h in range(1, HOPS[k] + 1))
-RELAYS = tuple((k, h) for h in (1, 2) for k in (3, 5, 2, 6) if HOPS[k] > h)
+LEGS = ((), (1,), (2,), (2, 1), (0, 0), (-2, -1), (-2,), (-1,))
+FIRST = (4, 3, 5, 2, 6, 1, 7)
+RELAYS = (4, 3, 5)
+ARRIVALS = tuple((k, h) for k in range(1, 8) for h in range(len(LEGS[k])))
 PLACE = (0, 1, 3, 5, 7, 6, 4, 2)
 
 
@@ -31,12 +31,12 @@
     home_hbm, slots_hbm, down_hbm,
     ids_ref, gw_ref, tok_ref, cot_ref, in_sem,
     wg, wu, wd, w_sem,
-    a_src, a_relay, a_dst, a_send, a_recv, far_relay, far_send, far_recv,
+    a_src, a_relay, a_dst, a_send, a_recv,
     xg, b_zsend, b_zrecv, b_xsend, b_xrecv,
     p_mine, d1_dst, d1_send, d1_recv,
     d2_own, d2_src, d2_dst, d2_send, d2_recv,
     h_all, d3_send, d3_recv, d4_send, d4_recv,
-    f_mine, f_src, f_dst, f_send, f_recv,
+    f_src, f_dst, f_send, f_recv,
     z_sum, z_src, z_dst, z_send, z_recv,
     g_src, g_send, g_recv,
     slot_buf, hid_buf, dy_buf, down_buf, out_sem,
@@ -85,18 +85,11 @@
         kept[-1].start()
 
     barrier = pltpu.get_barrier_semaphore()
-    far_way = 1 - 2 * ((group + 2) % EXPERTS // 4)
-    relays_far = 1 - group // 4
-    peers = [at_group(step) for step in (2 * far_way, 1, -1)] + [partner]
+    peers = [at_group(step) for step in (2, -2, 1, -1)] + [partner]
     peers += [at_plane(p) for p in near_planes]
     peers += [at(step) for at in (at_x, at_y) for step in (2, 1, 3)]
     for peer in peers:
         pl.semaphore_signal(barrier, inc=1, device_id=peer, device_id_type=MESH)
-
-    @pl.when(relays_far == 1)
-    def _():
-        pl.semaphore_signal(barrier, inc=1, device_id=at_group(-2 * far_way), device_id_type=MESH)
-
     inputs = [
         pltpu.make_async_copy(src, dst, in_sem.at[i])
         for i, (src, dst) in enumerate(
@@ -150,32 +143,16 @@
     slot_buf[1] = chosen
     local(slot_buf, slots_hbm, out_sem.at[1])
 
-    pl.semaphore_wait(barrier, len(peers) + relays_far)
+    pl.semaphore_wait(barrier, len(peers))
 
     def a_copy(k, h):
-        src = a_src.at[k] if h == 1 else a_relay.at[RELAYS.index((k, h - 1))]
-        dst = a_dst.at[PLACE[k]] if h == HOPS[k] else a_relay.at[RELAYS.index((k, h))]
+        src = a_relay.at[RELAYS.index(k)] if h else a_src.at[k]
+        dst = a_dst.at[PLACE[k]] if h == len(LEGS[k]) - 1 else a_relay.at[RELAYS.index(k)]
         n = ARRIVALS.index((k, h))
-        return remote(src, dst, a_send.at[n], a_recv.at[n], at_group(AHEAD[k]))
-
-    def a_far(way):
-        n = (1 - way) // 2
-        return remote(a_src.at[4], far_relay.at[n], far_send.at[2], far_recv.at[n], at_group(2 * way))
-
-    def a_far_end(way):
-        n = (1 - way) // 2
-        return remote(
-            far_relay.at[n], a_dst.at[PLACE[4]], far_send.at[n], far_recv.at[2], at_group(2 * way)
-        )
-
-    def a_pass(hop):
-        for k, h in RELAYS:
-            if h == hop:
-                a_copy(k, h).wait_recv()
-                start(a_copy(k, h + 1))
+        return remote(src, dst, a_send.at[n], a_recv.at[n], at_group(LEGS[k][h] or 2 * side))
 
     def a_end(k):
-        (a_copy(k, HOPS[k]) if HOPS[k] else a_far_end(1)).wait_recv()
+        a_copy(k, len(LEGS[k]) - 1).wait_recv()
 
     cap_rows = EXPERTS * CAP
     part_rows = cap_rows // 2
@@ -286,7 +263,7 @@
 
     def f(c, step):
         n = step - 1
-        return remote(f_src.at[c, n], f_dst.at[c, n], f_send.at[c, n], f_recv.at[c, n], at_x(step))
+        return remote(f_src.at[c, (x + step) % xs], f_dst.at[c, n], f_send.at[c, n], f_recv.at[c, n], at_x(step))
 
     def results(c):
         for step in range(4):
@@ -301,9 +278,8 @@
         )
         for i in range(4):
             cols = slice(i * feat, (i + 1) * feat)
-            f_mine[c, i] = jnp.concatenate([out_rows[:, cols], grad_rows[:, cols]], axis=1)
+            f_src[c, i] = jnp.concatenate([out_rows[:, cols], grad_rows[:, cols]], axis=1).astype(BF16)
         for step in (2, 1, 3):
-            f_src[c, step - 1] = f_mine[c, (x + step) % xs].astype(BF16)
             start(f(c, step))
         rows = pl.ds(c * half, half)
         hid_buf[rows, :] = hidden_all
@@ -313,7 +289,7 @@
         return remote(z_src.at[c, n], z_dst.at[c, n], z_send.at[c, n], z_recv.at[c, n], at_plane(order[j]))
 
     def sum_x(c):
-        chunk_sum = f_mine[c, x]
+        chunk_sum = f_src[c, x].astype(F32)
         for step in (1, 3, 2):
             f(c, step).wait_recv()
             chunk_sum = chunk_sum + f_dst[c, step - 1].astype(F32)
@@ -337,18 +313,11 @@
         for k in (4, 3, 5, 6) if c else (2, 1, 7):
             start(gc(k, -1))
 
-    start(a_far(far_way))
-    for k in (3, 5, 2, 6, 1, 7):
+    for k in FIRST:
+        start(a_copy(k, 0))
+    for k in RELAYS:
+        a_copy(k, 0).wait_recv()
         start(a_copy(k, 1))
-    a_pass(1)
-
-    @pl.when(relays_far == 1)
-    def _():
-        for way in (1, -1):
-            a_far(way).wait_recv()
-            a_far_end(way).start()
-
-    a_pass(2)
     for k in (1, 7, 2):
         a_end(k)
     gather(0)
@@ -378,12 +347,6 @@
     local(down_buf, down_hbm, out_sem.at[2])
     for copy in sent:
         copy.wait_send()
-
-    @pl.when(relays_far == 1)
-    def _():
-        for way in (1, -1):
-            a_far_end(way).wait_send()
-
     for copy in kept:
         copy.wait()
     for k in range(1, 8):
@@ -451,7 +414,6 @@
             pltpu.VMEM((units, wide), BF16), dma((3,)),
             pltpu.VMEM(block, BF16), pltpu.VMEM((len(RELAYS),) + block[1:], BF16),
             pltpu.VMEM(block, BF16), dma((len(ARRIVALS),)), dma((len(ARRIVALS),)),
-            pltpu.VMEM((2,) + block[1:], BF16), dma((3,)), dma((3,)),
             pltpu.VMEM((4, 2, planes, part, 2 * feat), BF16),
             dma((2, 3)), dma((2, 3)), dma((2, 4, 3)), dma((2, 4, 3)),
             pltpu.VMEM((2, 4, half, 384), F32), pltpu.VMEM((2, 4, half // 2, 384), F32), dma((2, 4)), dma((2, 4)),
@@ -459,7 +421,7 @@
             pltpu.VMEM((2, 3, half // 2, 384), BF16), pltpu.VMEM((2, 3, half // 2, 384), BF16),
             dma((2, 3)), dma((2, 3)),
             pltpu.VMEM((2, 4, 2, half // 2, 384), BF16), dma((2, 3)), dma((2, 3)), dma((2, 4)), dma((2, 4)),
-            pltpu.VMEM((2, 4, half, 2 * feat), F32), pltpu.VMEM((2, 3, half, 2 * feat), BF16),
+            pltpu.VMEM((2, 4, half, 2 * feat), BF16),
             pltpu.VMEM((2, 3, half, 2 * feat), BF16), dma((2, 3)), dma((2, 3)),
             pltpu.VMEM((2, planes, part, 2 * feat), F32),
             pltpu.VMEM((2, 3, part, 2 * feat), BF16), pltpu.VMEM((2, 3, part, 2 * feat), BF16),

time: 87.9 us -> 87.1 us (level)
  Pallas kernels: 87.1 us -> 86.2 us
where the time goes in v7:
time: 87.1 us; the launch traced here: 86.9 us
  Pallas kernels  86.2 us (99%)
    pallas_call x1, Pallas kernels, per_device(): pl.pallas_call(kernel, out_shape=(jax.ShapeDtypeStruct(block, BF16), jax....  84 us
    pallas_call x1, Pallas kernels, per_device(): pl.pallas_call(finish, out_shape=(jax.ShapeDtypeStruct((tok_rows, feat),...  2.23 us

profile of v7, /device:TPU:1, one launch (start us, length us, event | category | flops | bytes accessed | tf_op | source)
XLA Modules:
  0.0 86.9 jit_solution(6548904219773364639)
XLA Ops:
  0.6 84.0 %shard_map.94 = (bf16[8,8,384]{2,1,0:T(8,128)(2,1)}, f32[2,64,16]{2,1,0:T(8,128)}, bf16[512,768]{1,0:T(8,128)(2,1)}) custom-call(s32[2,16]{1,0:T(2,128)} %bitcast.2, f32[2,16]{1,0:T(2,128)} %bitcast.3, bf16[16,192]{1,0:T(8,128)(2,1)} %tok_hbm.1, bf16[16,192]{1,0:T(8,128)(2,1)} %cot_hbm.1, bf16[768,512]{1,0:T(8,128)(2,1)} %wg_hbm.1, bf16[768,512]{1,0:T(8,128)(2,1)} %wu_hbm.1, ...), custom_call_target="tpu_custom_call" | custom-call | tf_op jit(solution)/shard_map/pallas_call | solution.py:401
  84.6 2.2 %shard_map.95 = (bf16[16,192]{1,0:T(8,128)(2,1)}, bf16[16,192]{1,0:T(8,128)(2,1)}, bf16[512,768]{1,0:T(8,128)(2,1)}) custom-call(bf16[8,8,384]{2,1,0:T(8,128)(2,1)} %get-tuple-element.6.home_hbm, f32[2,64,16]{2,1,0:T(8,128)} %get-tuple-element.7.slots_hbm, bf16[512,768]{1,0:T(8,128)(2,1)} %get-tuple-element.8.made_hbm), custom_call_target="tpu_custom_call" | custom-call | tf_op jit(solution)/shard_map/pallas_call | solution.py:436

commit v8 on v7

--- a/solution.py
+++ b/solution.py
@@ -63,9 +63,9 @@
     def at_x(step):
         return {"tpout": (x + step + xs) % xs}
 
-    def at_y(step):
+    def at_y(step, other=0):
         there = (y + step + 4) % 4
-        return {"tpin": there // 2, "dp": (there % 2) * 2 + core}
+        return {"tpin": there // 2, "dp": (there % 2) * 2 + (core + other) % 2}
 
     partner = {"dp": dp + side}
     near_planes = (plane + 1 - 2 * (plane % 2), (plane + 2) % 4, 3 - plane)
@@ -88,6 +88,7 @@
     peers = [at_group(step) for step in (2, -2, 1, -1)] + [partner]
     peers += [at_plane(p) for p in near_planes]
     peers += [at(step) for at in (at_x, at_y) for step in (2, 1, 3)]
+    peers += [at_y(step, 1) for step in (2, 1, 3)]
     for peer in peers:
         pl.semaphore_signal(barrier, inc=1, device_id=peer, device_id_type=MESH)
     inputs = [
@@ -233,13 +234,23 @@
             start(d2(c, step))
         d2_own[c] = pair_sum(c, 0)
 
-    def d3(c, step, whose):
+    def d3(c, step, other, whose):
         there = h_all.at[c, whose, core]
-        return remote(there, there, d3_send.at[c, step - 1], d3_recv.at[c, step - 1], at_y(step))
-
-    def d4(c, step, whose):
-        there = h_all.at[c, wrap_y[step], whose]
-        return remote(there, there, d4_send.at[c, step], d4_recv.at[c, step], partner)
+        n = step - 1
+        return remote(
+            there, there, d3_send.at[c, other, n], d3_recv.at[c, other, n], at_y(step, other)
+        )
+
+    def d3_in(c, step, other):
+        there = h_all.at[c, wrap_y[4 - step], (core + other) % 2]
+        n = step - 1
+        return remote(
+            there, there, d3_send.at[c, other, n], d3_recv.at[c, other, n], at_y(step, other)
+        )
+
+    def d4(c, whose):
+        there = h_all.at[c, y, whose]
+        return remote(there, there, d4_send.at[c], d4_recv.at[c], partner)
 
     def activate(c):
         total = d2_own[c]
@@ -253,21 +264,19 @@
         up_grad = (hidden_grad * gate * sig).astype(BF16)
         h_all[c, y, core] = jnp.concatenate([hidden, gate_grad, up_grad], axis=1)
         for step in (2, 1, 3):
-            start(d3(c, step, y))
-        start(d4(c, 0, core))
-
-    def spread_core(c):
-        for step in (1, 3, 2):
-            d3(c, step, wrap_y[4 - step]).wait_recv()
-            start(d4(c, 4 - step, core))
+            for other in (1, 0):
+                start(d3(c, step, other, y))
+        start(d4(c, core))
 
     def f(c, step):
         n = step - 1
         return remote(f_src.at[c, (x + step) % xs], f_dst.at[c, n], f_send.at[c, n], f_recv.at[c, n], at_x(step))
 
     def results(c):
-        for step in range(4):
-            d4(c, step, 1 - core).wait_recv()
+        d4(c, 1 - core).wait_recv()
+        for step in (1, 3, 2):
+            for other in (0, 1):
+                d3_in(c, step, other).wait_recv()
         acts = [h_all[c, i].reshape(half, 384) for i in range(4)]
         hidden_all = jnp.concatenate([a[:, :128] for a in acts], axis=1)
         gate_grad_all = jnp.concatenate([a[:, 128:256] for a in acts], axis=1)
@@ -333,11 +342,9 @@
     activate(0)
     products(1)
     sum_cores(1)
-    spread_core(0)
     results(0)
     activate(1)
     sum_x(0)
-    spread_core(1)
     results(1)
     go_home(0)
     local(g_src.at[0], home_hbm.at[0], out_sem.at[0])
@@ -420,7 +427,7 @@
             pltpu.VMEM((2, half // 2, 384), F32),
             pltpu.VMEM((2, 3, half // 2, 384), BF16), pltpu.VMEM((2, 3, half // 2, 384), BF16),
             dma((2, 3)), dma((2, 3)),
-            pltpu.VMEM((2, 4, 2, half // 2, 384), BF16), dma((2, 3)), dma((2, 3)), dma((2, 4)), dma((2, 4)),
+            pltpu.VMEM((2, 4, 2, half // 2, 384), BF16), dma((2, 2, 3)), dma((2, 2, 3)), dma((2,)), dma((2,)),
             pltpu.VMEM((2, 4, half, 2 * feat), BF16),
             pltpu.VMEM((2, 3, half, 2 * feat), BF16), dma((2, 3)), dma((2, 3)),
             pltpu.VMEM((2, planes, part, 2 * feat), F32),

time: 87.1 us -> 86 us (0.987)
  Pallas kernels: 86.2 us -> 85.2 us
    pallas_call x1, Pallas kernels: 84 us -> 82.9 us  [per_device(): pl.pallas_call(kernel, out_shape=(jax.ShapeDtypeStruct(block, BF16), jax....]
where the time goes in v8:
time: 86 us; the launch traced here: 85.8 us
  Pallas kernels  85.2 us (99%)
    pallas_call x1, Pallas kernels, per_device(): pl.pallas_call(kernel, out_shape=(jax.ShapeDtypeStruct(block, BF16), jax....  82.9 us
    pallas_call x1, Pallas kernels, per_device(): pl.pallas_call(finish, out_shape=(jax.ShapeDtypeStruct((tok_rows, feat),...  2.23 us

profile of v8, /device:TPU:1, one launch (start us, length us, event | category | flops | bytes accessed | tf_op | source)
XLA Modules:
  0.0 85.8 jit_solution(8558539962433530469)
XLA Ops:
  0.6 82.9 %shard_map.94 = (bf16[8,8,384]{2,1,0:T(8,128)(2,1)}, f32[2,64,16]{2,1,0:T(8,128)}, bf16[512,768]{1,0:T(8,128)(2,1)}) custom-call(s32[2,16]{1,0:T(2,128)} %bitcast.2, f32[2,16]{1,0:T(2,128)} %bitcast.3, bf16[16,192]{1,0:T(8,128)(2,1)} %tok_hbm.1, bf16[16,192]{1,0:T(8,128)(2,1)} %cot_hbm.1, bf16[768,512]{1,0:T(8,128)(2,1)} %wg_hbm.1, bf16[768,512]{1,0:T(8,128)(2,1)} %wu_hbm.1, ...), custom_call_target="tpu_custom_call" | custom-call | tf_op jit(solution)/shard_map/pallas_call | solution.py:408
  83.6 2.2 %shard_map.95 = (bf16[16,192]{1,0:T(8,128)(2,1)}, bf16[16,192]{1,0:T(8,128)(2,1)}, bf16[512,768]{1,0:T(8,128)(2,1)}) custom-call(bf16[8,8,384]{2,1,0:T(8,128)(2,1)} %get-tuple-element.6.home_hbm, f32[2,64,16]{2,1,0:T(8,128)} %get-tuple-element.7.slots_hbm, bf16[512,768]{1,0:T(8,128)(2,1)} %get-tuple-element.8.made_hbm), custom_call_target="tpu_custom_call" | custom-call | tf_op jit(solution)/shard_map/pallas_call | solution.py:443
